TPU v7x, 32 devices: a whole 2x2x4 slice. The times are simulated.
32 devices in a mesh: parts: 2 (over x), owner: 16 (over z, y, core).
Axes of the slice: x: 2, y: 2, z: 4, core: 2. Of those that a mesh axis runs over, the one named last changes fastest.
Arguments:
- embeddings: bfloat16 [32768, 768], P(('parts', 'owner')), parts along dimension 0, may hold values from -6 to 6
- cluster_ids: int32 [32768], P(('parts', 'owner')), parts along dimension 0, may hold values from 0 to 63, as said below
- owner_map: int32 [128], P('parts'), parts along dimension 0, may hold values from 0 to 15, as said below
Outputs:
- maxima: float32 [32768], P(('parts', 'owner')), parts along dimension 0
- cluster_mean: float32 [128], P('parts'), parts along dimension 0
There are 2 independent parts, one for each index of `parts`. A program takes and returns all parts, laid end to end along the dimension named above; each array names one. Nothing has to cross between parts.
Inputs may be any that keep to these rules, and one draw needn't show every extreme that they name: `cluster_ids`: cluster of each item. Owners 2k and 2k+1 form a pair; exactly 128 of the items of one device belong to clusters of one pair, so at most 128 to one owner, and in every draw some owner receives exactly 128 items from every device. `owner_map`: every owner owns exactly 4 clusters.
All inputs are finite; a program needn't handle non-finite values.
Results may differ from a plain program's by a relative error of at most 0.0015.
Values may be sent and summed in bfloat16 or wider, within the bound.
No kernel may reach another device: no remote copies, remote signals or barrier semaphores. Data moves between devices by JAX's collectives and lax.ppermute only.
A program may use at most 64 MiB of HBM per device.

v0:
```python
import functools

import jax
import jax.numpy as jnp
from jax import lax
from jax.experimental import pallas as pl
from jax.experimental.pallas import tpu as pltpu
from jax.sharding import PartitionSpec as P


LANES = 128
EXTRA = 16
F32 = jnp.float32
BF16 = jnp.bfloat16
VMEM = pl.BlockSpec(memory_space=pltpu.VMEM)
HBM = pl.BlockSpec(memory_space=pltpu.HBM)
PARAMS = pltpu.CompilerParams(vmem_limit_bytes=16 * 2**20)


def iota(shape, dim):
    return lax.broadcasted_iota(jnp.int32, shape, dim)


def near(value):
    return pltpu.with_memory_space_constraint(value, pltpu.VMEM)


def far(value):
    return pltpu.with_memory_space_constraint(value, pltpu.HBM)


def lane_take(row, index):
    if index.shape[0] == 1:
        return lane_take(row, jnp.broadcast_to(index, (8, LANES)))[0:1, :]
    out = None
    for first in range(0, row.shape[1], LANES):
        piece = jnp.broadcast_to(row[:, first : first + LANES], index.shape)
        local = index - first
        inside = (local >= 0) & (local < LANES)
        taken = jnp.take_along_axis(
            piece, jnp.where(inside, local, 0), axis=1, mode="promise_in_bounds"
        )
        out = taken if out is None else jnp.where(inside, taken, out)
    return out


def route(ids_ref, owners_ref, pair_ref, rank_ref, label_ref, table_ref, slot_ref, pad, pairs, clusters):
    chip = lax.axis_index("owner") // 2
    chunks = ids_ref.shape[0]
    padded = pad.shape[1]
    pad[...] = jnp.full(pad.shape, -2, jnp.int32)
    pad[0:1, 0:clusters] = owners_ref[...]
    pair_row = pad[0:1, :] >> 1
    across = jnp.broadcast_to(pair_row, (padded, padded))
    down = across.astype(F32).T.astype(jnp.int32)
    before = (across == down) & (iota(across.shape, 0) < iota(across.shape, 1))
    local_row = jnp.sum(before.astype(F32), axis=0, keepdims=True).astype(jnp.int32)
    table_ref[0:1, :] = pair_row
    table_ref[1:2, :] = local_row
    ids = ids_ref[...]
    pair = lane_take(pair_row, ids)
    label_ref[...] = lane_take(local_row, ids).astype(F32)
    hots = [pair == (chip ^ m) for m in range(pairs)]
    hot = jnp.concatenate([h.astype(F32) for h in hots], axis=0)
    upper = (iota((LANES, LANES), 0) <= iota((LANES, LANES), 1)).astype(BF16)
    within = jnp.dot(hot.astype(BF16), upper, preferred_element_type=F32)
    sums = jnp.dot(hot.astype(BF16), jnp.ones((LANES, LANES), BF16), preferred_element_type=F32)
    r, c = iota((pairs * chunks,) * 2, 0), iota((pairs * chunks,) * 2, 1)
    earlier = ((r // chunks == c // chunks) & (c < r)).astype(BF16)
    offset = jnp.dot(earlier, sums.astype(BF16), preferred_element_type=F32)
    slot = jnp.where(hot > 0.0, within + offset - 1.0, -1.0)
    item_rank = slot[0:chunks, :]
    for m in range(1, pairs):
        item_rank = jnp.maximum(item_rank, slot[m * chunks : (m + 1) * chunks, :])
    slot_ref[...] = slot
    pair_ref[...] = pair
    rank_ref[...] = item_rank.astype(jnp.int32)


def pack(slot_ref, label_ref, rows, blocks, numbers, capacity):
    chunks = label_ref.shape[0]
    width = rows.shape[1]
    slabs = width // LANES
    label = jnp.concatenate([label_ref[k : k + 1, :] for k in range(chunks)], axis=1)
    label = jnp.broadcast_to(label, (EXTRA, chunks * LANES)).astype(BF16)
    place = iota((capacity, LANES), 0).astype(F32)
    for block, m in zip(blocks, numbers):
        chosen = jnp.concatenate(
            [
                (place == slot_ref[m * chunks + k : m * chunks + k + 1, :]).astype(F32).astype(BF16)
                for k in range(chunks)
            ],
            axis=1,
        )
        values = jnp.dot(chosen, rows[...], preferred_element_type=F32)
        scale = lax.rsqrt(jnp.mean(values * values, axis=1, keepdims=True) + 1e-06)
        unit = (values * scale * (1.0 / jnp.sqrt(F32(width)))).astype(BF16)
        labels = lax.dot_general(
            label, chosen, (((1,), (1,)), ((), ())), preferred_element_type=F32
        )
        for k in range(slabs):
            block[k * capacity : (k + 1) * capacity, :] = unit[:, k * LANES : (k + 1) * LANES]
        block[slabs * capacity : slabs * capacity + EXTRA, 0:capacity] = labels.astype(BF16)


def first_kernel(ids_hbm, owners_hbm, rows_hbm, *refs, numbers, pairs, capacity, clusters):
    n = len(numbers)
    blocks = refs[:n]
    pair_ref, rank_ref, label_ref, table_ref, slot_ref, rows, ids_ref, owners_ref, pad, sems = refs[n:]
    copies = [
        pltpu.make_async_copy(source, target, sems.at[k])
        for k, (source, target) in enumerate(
            ((ids_hbm, ids_ref), (owners_hbm, owners_ref), (rows_hbm, rows))
        )
    ]
    for copy in copies:
        copy.start()
    copies[0].wait()
    copies[1].wait()
    route(ids_ref, owners_ref, pair_ref, rank_ref, label_ref, table_ref, slot_ref, pad, pairs, clusters)
    copies[2].wait()
    pack(slot_ref, label_ref, rows, blocks, numbers, capacity)


def first_blocks(ids, owners, rows, numbers, pairs, capacity):
    clusters = owners.shape[1]
    padded = -(-clusters // LANES) * LANES
    height = rows.shape[1] // LANES * capacity + EXTRA
    return pl.pallas_call(
        functools.partial(
            first_kernel, numbers=numbers, pairs=pairs, capacity=capacity, clusters=clusters
        ),
        in_specs=[HBM] * 3,
        out_specs=[VMEM] * (len(numbers) + 6),
        out_shape=[pltpu.VMEM((height, LANES), BF16)] * len(numbers)
        + [
            pltpu.VMEM(ids.shape, jnp.int32),
            pltpu.VMEM(ids.shape, jnp.int32),
            pltpu.VMEM(ids.shape, F32),
            pltpu.VMEM((8, padded), jnp.int32),
            pltpu.VMEM((pairs * ids.shape[0], LANES), F32),
            pltpu.VMEM(rows.shape, BF16),
        ],
        scratch_shapes=[
            pltpu.VMEM(ids.shape, jnp.int32),
            pltpu.VMEM(owners.shape, jnp.int32),
            pltpu.VMEM((8, padded), jnp.int32),
            pltpu.SemaphoreType.DMA((3,)),
        ],
        name="first",
        compiler_params=PARAMS,
    )(far(ids), far(owners), far(rows))


def later_kernel(slot_ref, label_ref, rows_ref, *blocks, numbers, capacity):
    pack(slot_ref, label_ref, rows_ref, blocks, numbers, capacity)


def later_blocks(slot, label, rows, numbers, capacity):
    height = rows.shape[1] // LANES * capacity + EXTRA
    return pl.pallas_call(
        functools.partial(later_kernel, numbers=numbers, capacity=capacity),
        in_specs=[VMEM] * 3,
        out_specs=[VMEM] * len(numbers),
        out_shape=[pltpu.VMEM((height, LANES), BF16)] * len(numbers),
        name="later",
        compiler_params=PARAMS,
    )(near(slot), near(label), near(rows))


def stage_kernel(*refs, old, new, capacity, width, last):
    slabs = width // LANES
    group = LANES // capacity
    total = old + new
    refs = list(refs)
    blocks = [refs.pop(0) for _ in range(2 * total)]
    best_in = refs.pop(0) if old else None
    out_ref, keys, marks = refs
    for b, block in enumerate(blocks):
        at = b * capacity
        for k in range(slabs):
            keys[at : at + capacity, k * LANES : (k + 1) * LANES] = block[
                k * capacity : (k + 1) * capacity, :
            ]
        marks[0:1, at : at + capacity] = block[
            slabs * capacity : slabs * capacity + EXTRA, 0:capacity
        ].astype(F32)[0:1, :]
    tiles, old_tiles = total // group, old // group
    best = [best_in[:, t * LANES : (t + 1) * LANES] for t in range(old_tiles)]
    best += [jnp.full((8, LANES), -1.0, F32)] * (tiles - old_tiles)

    def span(first, stop):
        return slice(first * LANES, stop * LANES)

    def visit(key_first, key_stop, first, stop):
        for left in range(key_first, key_stop, 2):
            right = min(left + 2, key_stop)
            gram = lax.dot_general(
                keys[span(left, right), :],
                keys[span(first, stop), :],
                (((1,), (1,)), ((), ())),
                preferred_element_type=F32,
            )
            for key in range(left, right):
                column = jnp.broadcast_to(marks[0:1, span(key, key + 1)], (LANES, LANES)).T
                for t in range(first, stop):
                    same = column == marks[0:1, span(t, t + 1)]
                    if t == key:
                        same = same & (iota((LANES, LANES), 0) != iota((LANES, LANES), 1))
                    piece = gram[span(key - left, key - left + 1), span(t - first, t - first + 1)]
                    piece = jnp.where(same, piece, -1.0)
                    top = jnp.max(piece.reshape(LANES // 8, 8, LANES), axis=0)
                    best[t] = jnp.maximum(best[t], top)

    visit(0, 2 * tiles, old_tiles, tiles)
    if old:
        visit(old_tiles, tiles, 0, old_tiles)
        visit(tiles + old_tiles, 2 * tiles, 0, old_tiles)
    if last is None:
        for t in range(tiles):
            out_ref[:, span(t, t + 1)] = best[t]
        return
    numbers, per_pair = last
    pairs = len(numbers)
    owner = lax.axis_index("owner")
    chip, core = owner // 2, owner % 2
    rows = [jnp.max(b, axis=0, keepdims=True) for b in best]
    row = jnp.concatenate(rows, axis=0)
    mark = jnp.concatenate([marks[0:1, span(t, t + 1)] for t in range(tiles)], axis=0)
    sums, counts = [], []
    for k in range(per_pair):
        mine = mark == k
        sums.append(jnp.sum(jnp.where(mine, row, 0.0), axis=0, keepdims=True))
        counts.append(jnp.sum(mine.astype(F32), axis=0, keepdims=True))
    stats = jnp.sum(jnp.concatenate(sums + counts, axis=0), axis=1, keepdims=True)
    stats = jnp.concatenate(
        [
            jnp.broadcast_to(stats, (2 * per_pair, LANES)),
            jnp.zeros((LANES - 2 * per_pair, LANES), F32),
        ],
        axis=0,
    ).T[0:1, :]
    for d in range(2 * pairs):
        out_ref[d, 1:2, :] = stats
    for t in range(tiles):
        marks[1:2, span(t, t + 1)] = rows[t]
    for b, m in enumerate(numbers):
        out_ref[2 * (chip ^ m) + core, 0:1, 0:capacity] = marks[
            1:2, b * capacity : (b + 1) * capacity
        ]


def stage(own, other, old, best, width, capacity, last):
    total = len(own)
    if last is None:
        out = pltpu.VMEM((8, total * capacity), F32)
    else:
        out = jax.ShapeDtypeStruct((2 * total, 8, LANES), F32)
    args = [near(b) for b in own] + [near(b) for b in other]
    if old:
        args.append(near(best))
    return pl.pallas_call(
        functools.partial(
            stage_kernel, old=old, new=total - old, capacity=capacity, width=width, last=last
        ),
        in_specs=[VMEM] * len(args),
        out_specs=VMEM,
        out_shape=out,
        scratch_shapes=[
            pltpu.VMEM((2 * total * capacity, width), BF16),
            pltpu.VMEM((8, 2 * total * capacity), F32),
        ],
        name="stage",
        compiler_params=PARAMS,
    )(*args)


def finish_kernel(back_ref, pair_ref, rank_ref, table_ref, maxima_ref, mean_ref, *, pairs, per_pair):
    core = lax.axis_index("owner") % 2
    pair, rank = pair_ref[...], rank_ref[...]
    maxima = jnp.zeros(pair.shape, F32)
    padded = table_ref.shape[1]
    pair_row, local_row = table_ref[0:1, :], table_ref[1:2, :]
    total = jnp.zeros((1, padded), F32)
    number = jnp.zeros((1, padded), F32)
    for p in range(pairs):
        got = lane_take(back_ref[2 * p + core, 0:1, :], rank)
        maxima = jnp.where(pair == p, got, maxima)
        stats = back_ref[2 * p, 1:2, :] + back_ref[2 * p + 1, 1:2, :]
        mine = pair_row == p
        index = jnp.where(mine, local_row, 0)
        parts = [index[:, f : f + LANES] for f in range(0, padded, LANES)]
        sums = jnp.concatenate([lane_take(stats, i) for i in parts], axis=1)
        counts = jnp.concatenate([lane_take(stats, i + per_pair) for i in parts], axis=1)
        total = jnp.where(mine, sums, total)
        number = jnp.where(mine, counts, number)
    maxima_ref[...] = maxima
    mean = total / jnp.maximum(number, 1.0)
    mean_ref[...] = mean[:, : mean_ref.shape[1]]


def finish(back, pair, rank, table, clusters, pairs, per_pair):
    return pl.pallas_call(
        functools.partial(finish_kernel, pairs=pairs, per_pair=per_pair),
        in_specs=[VMEM] * 4,
        out_specs=[VMEM] * 2,
        out_shape=[
            jax.ShapeDtypeStruct(pair.shape, F32),
            jax.ShapeDtypeStruct((1, clusters), F32),
        ],
        name="finish",
        compiler_params=PARAMS,
    )(back, near(pair), near(rank), near(table))


def plan(pairs):
    quarter = pairs // 4
    parts = [list(range(hi * quarter, (hi + 1) * quarter)) for hi in range(4)]
    sent = parts[3] + parts[2] + parts[1] + parts[0]
    stages = [parts[3] + parts[0][:1], parts[1] + parts[0][1:], parts[2]]
    return sent, quarter, stages


def body(embeddings, cluster_ids, owner_map):
    owners = lax.axis_size("owner")
    items, width = embeddings.shape
    clusters = owner_map.shape[0]
    pairs = owners // 2
    capacity = items // pairs
    per_pair = clusters // pairs
    ids = cluster_ids.reshape(items // LANES, LANES)
    sent, head, stages = plan(pairs)
    *blocks, pair, rank, label, table, slot, rows = first_blocks(
        ids, owner_map.reshape(1, clusters), embeddings, sent[:head], pairs, capacity
    )
    blocks += later_blocks(slot, label, rows, sent[head:], capacity)
    blocks = dict(zip(sent, blocks))
    swap = [(d, d ^ 1) for d in range(owners)]
    own = {}
    for m in sent:
        own[m] = blocks[m]
        if m:
            own[m] = lax.ppermute(own[m], "owner", [(d, d ^ (2 * m)) for d in range(owners)])
    other = {}
    done, best = [], None
    for index, new in enumerate(stages):
        for m in new:
            other[m] = lax.ppermute(own[m], "owner", swap)
        numbers = done + new
        last = (tuple(numbers), per_pair) if index == len(stages) - 1 else None
        best = stage(
            [own[m] for m in numbers],
            [other[m] for m in numbers],
            len(done),
            best,
            width,
            capacity,
            last,
        )
        done = numbers
    back = lax.all_to_all(best, "owner", split_axis=0, concat_axis=0, tiled=True)
    maxima, mean = finish(back, pair, rank, table, clusters, pairs, per_pair)
    return maxima.reshape(items), mean.reshape(clusters)


def solution(mesh):
    placed = (P(("parts", "owner"), None), P(("parts", "owner")), P("parts"))
    return jax.shard_map(
        body,
        mesh=mesh,
        in_specs=placed,
        out_specs=(P(("parts", "owner")), P("parts")),
        check_vma=False,
    )
```

profile of v0, /device:TPU:0, one launch (start us, length us, event | category | flops | bytes accessed | tf_op | source)
XLA Modules:
  0.0 65.2 jit_solution(13334927580982609006)
XLA Ops:
  0.6 2.3 %first.1 = (bf16[784,128]{1,0:T(8,128)(2,1)S(1)}, bf16[784,128]{1,0:T(8,128)(2,1)S(1)}, s32[8,128]{1,0:T(8,128)S(1)}, s32[8,128]{1,0:T(8,128)S(1)}, f32[8,128]{1...) custom-call(s32[8,128]{1,0:T(8,128)} %bitcast.4, s32[1,64]{1,0:T(1,128)} %bitcast.5, ...), custom_call_target="tpu_custom_call" | custom-call | tf_op jit(solution)/shard_map/first/pallas_call | solution.py:129
  2.9 2.0 %later.1 = (bf16[784,128]{1,0:T(8,128)(2,1)S(1)}, bf16[784,128]{1,0:T(8,128)(2,1)S(1)}, bf16[784,128]{1,0:T(8,128)(2,1)S(1)}, bf16[784,128]{1,0:T(8,128)(2,1)S(1...) custom-call(f32[64,128]{1,0:T(8,128)S(1)} %get-tuple-element.20.slot_ref, ...), custom_call_target="tpu_custom_call" | custom-call | tf_op jit(solution)/shard_map/later/pallas_call | solution.py:161
  4.9 0.6 collective-permute-start.9
  5.5 4.7 %collective-permute-start = (bf16[784,128]{1,0:T(8,128)(2,1)S(1)}, bf16[784,128]{1,0:T(8,128)(2,1)S(1)}, u32[]{:S(2)}, u32[]{:S(2)}) collective-permute-start(bf16[784,128]{1,0:T(8,128)(2,1)S(1)} %get-tuple-element.18), channel_id=1, source_target_pairs={{0,12},{1,13},{2,14},{3,15},{4,8},{5,9},{6,10},{7,11},{8,4},{9,5},... | collective-permute-start | bytes 602120 | tf_op jit(solution)/shard_map/ppermute | solution.py:343
  10.2 1.2 %collective-permute-start.1 = (bf16[784,128]{1,0:T(8,128)(2,1)S(1)}, bf16[784,128]{1,0:T(8,128)(2,1)S(1)}, u32[]{:S(2)}, u32[]{:S(2)}) collective-permute-start(bf16[784,128]{1,0:T(8,128)(2,1)S(1)} %get-tuple-element.19), channel_id=1, source_target_pairs={{0,14},{1,15},{2,12},{3,13},{4,10},{5,11},{6,8},{7,9},{8,6},{9,7},... | collective-permute-start | bytes 602120 | tf_op jit(solution)/shard_map/ppermute | solution.py:343
  11.3 0.0 collective-permute-start.2
  11.3 1.8 %collective-permute-start.3 = (bf16[784,128]{1,0:T(8,128)(2,1)S(1)}, bf16[784,128]{1,0:T(8,128)(2,1)S(1)}, u32[]{:S(2)}, u32[]{:S(2)}) collective-permute-start(bf16[784,128]{1,0:T(8,128)(2,1)S(1)} %get-tuple-element.25), channel_id=1, source_target_pairs={{0,6},{1,7},{2,4},{3,5},{4,2},{5,3},{6,0},{7,1},{8,14},{9,15},{10,... | collective-permute-start | bytes 602120 | tf_op jit(solution)/shard_map/ppermute | solution.py:343
  13.2 0.0 collective-permute-done.9.refs_5_.refs_8_.refs_10_
  13.2 1.7 %collective-permute-start.4 = (bf16[784,128]{1,0:T(8,128)(2,1)S(1)}, bf16[784,128]{1,0:T(8,128)(2,1)S(1)}, u32[]{:S(2)}, u32[]{:S(2)}) collective-permute-start(bf16[784,128]{1,0:T(8,128)(2,1)S(1)} %get-tuple-element.26), channel_id=1, source_target_pairs={{0,2},{1,3},{2,0},{3,1},{4,6},{5,7},{6,4},{7,5},{8,10},{9,11},{10,... | collective-permute-start | bytes 602120 | tf_op jit(solution)/shard_map/ppermute | solution.py:343
  14.8 1.2 %collective-permute-done.refs_0_ = bf16[784,128]{1,0:T(8,128)(2,1)S(1)} collective-permute-done((bf16[784,128]{1,0:T(8,128)(2,1)S(1)}, bf16[784,128]{1,0:T(8,128)(2,1)S(1)}, u32[]{:S(2)}, u32[]{:S(2)}) %collective-permute-start) | collective-permute-done | bytes 200736 | tf_op jit(solution)/shard_map/ppermute | solution.py:343
  16.1 9.5 %collective-permute-start.5 = (bf16[784,128]{1,0:T(8,128)(2,1)S(1)}, bf16[784,128]{1,0:T(8,128)(2,1)S(1)}, u32[]{:S(2)}, u32[]{:S(2)}) collective-permute-start(bf16[784,128]{1,0:T(8,128)(2,1)S(1)} %get-tuple-element.27), channel_id=1, source_target_pairs={{0,8},{1,9},{2,10},{3,11},{4,12},{5,13},{6,14},{7,15},{8,0},{9,1},... | collective-permute-start | bytes 602120 | tf_op jit(solution)/shard_map/ppermute | solution.py:343
  25.6 0.0 collective-permute-done.1.refs_1_
  25.6 8.3 %collective-permute-start.6 = (bf16[784,128]{1,0:T(8,128)(2,1)S(1)}, bf16[784,128]{1,0:T(8,128)(2,1)S(1)}, u32[]{:S(2)}, u32[]{:S(2)}) collective-permute-start(bf16[784,128]{1,0:T(8,128)(2,1)S(1)} %get-tuple-element.28), channel_id=1, source_target_pairs={{0,10},{1,11},{2,8},{3,9},{4,14},{5,15},{6,12},{7,13},{8,2},{9,3},... | collective-permute-start | bytes 602120 | tf_op jit(solution)/shard_map/ppermute | solution.py:343
  34.0 0.0 collective-permute-done.3.refs_4_
  34.0 0.5 collective-permute-start.8
  34.5 0.1 collective-permute-start.10
  34.5 7.5 %collective-permute-done.5.refs_6_ = bf16[784,128]{1,0:T(8,128)(2,1)S(1)} collective-permute-done((bf16[784,128]{1,0:T(8,128)(2,1)S(1)}, bf16[784,128]{1,0:T(8,128)(2,1)S(1)}, u32[]{:S(2)}, u32[]{:S(2)}) %collective-permute-start.5) | collective-permute-done | bytes 200736 | tf_op jit(solution)/shard_map/ppermute | solution.py:343
  42.1 0.0 collective-permute-start.11
  42.1 4.7 %collective-permute-done.6.refs_7_ = bf16[784,128]{1,0:T(8,128)(2,1)S(1)} collective-permute-done((bf16[784,128]{1,0:T(8,128)(2,1)S(1)}, bf16[784,128]{1,0:T(8,128)(2,1)S(1)}, u32[]{:S(2)}, u32[]{:S(2)}) %collective-permute-start.6) | collective-permute-done | bytes 200736 | tf_op jit(solution)/shard_map/ppermute | solution.py:343
  46.8 0.0 collective-permute-start.12
  46.8 0.0 collective-permute-done.7.refs_3_.refs_6_.refs_8_
  46.8 0.5 collective-permute-start.13
  47.3 0.1 collective-permute-start.14
  47.4 0.8 %stage.3.refs_12_ = f32[8,384]{1,0:T(8,128)S(1)} custom-call(bf16[784,128]{1,0:T(8,128)(2,1)S(1)} %collective-permute-done.refs_0_, bf16[784,128]{1,0:T(8,128)(2,1)S(1)} %collective-permute-done.1.refs_1_, bf16[784,128]{1,0:T(8,128)(2,1)S(1)} %get-tuple-element.23.refs_2_, bf16[784,128]{1,0:T(8,128)(2,1)S(1)} %collective-permute-done.7.refs_3_.refs_6_.refs_8_, ...), custom_call_target="tpu_custom_call" | custom-call | tf_op jit(solution)/shard_map/stage/pallas_call | solution.py:262
  48.2 0.0 collective-permute-done.10.refs_9_.refs_11_
  48.2 0.0 collective-permute-done.11.refs_10_.refs_12_
  48.2 0.0 collective-permute-done.12.refs_11_.refs_13_
  48.3 2.2 %stage.4.refs_16_ = f32[8,768]{1,0:T(8,128)S(1)} custom-call(bf16[784,128]{1,0:T(8,128)(2,1)S(1)} %collective-permute-done.refs_0_, bf16[784,128]{1,0:T(8,128)(2,1)S(1)} %collective-permute-done.1.refs_1_, bf16[784,128]{1,0:T(8,128)(2,1)S(1)} %get-tuple-element.23.refs_2_, bf16[784,128]{1,0:T(8,128)(2,1)S(1)} %collective-permute-done.2.refs_3_, ...), custom_call_target="tpu_custom_call" | custom-call | tf_op jit(solution)/shard_map/stage/pallas_call | solution.py:262
  50.5 0.0 collective-permute-done.13.refs_14_
  50.5 2.0 %stage.5 = f32[16,8,128]{2,1,0:T(8,128)S(1)} custom-call(bf16[784,128]{1,0:T(8,128)(2,1)S(1)} %collective-permute-done.refs_0_, bf16[784,128]{1,0:T(8,128)(2,1)S(1)} %collective-permute-done.1.refs_1_, bf16[784,128]{1,0:T(8,128)(2,1)S(1)} %get-tuple-element.23.refs_2_, bf16[784,128]{1,0:T(8,128)(2,1)S(1)} %collective-permute-done.2.refs_3_, ...), custom_call_target="tpu_custom_call" | custom-call | tf_op jit(solution)/shard_map/stage/pallas_call | solution.py:262
  52.5 12.0 %all_to_all.5.back_ref = f32[16,8,128]{2,1,0:T(8,128)S(1)} all-to-all(f32[16,8,128]{2,1,0:T(8,128)S(1)} %stage.5), channel_id=1, replica_groups=mesh['parts'=2,'owner'=16] {'owner'}, dimensions={0} | all-to-all | bytes 131072 | tf_op jit(solution)/shard_map/all_to_all | solution.py:361
  64.5 0.7 %finish.1 = (f32[8,128]{1,0:T(8,128)}, f32[1,64]{1,0:T(1,128)}) custom-call(f32[16,8,128]{2,1,0:T(8,128)S(1)} %all_to_all.5.back_ref, s32[8,128]{1,0:T(8,128)S(1)} %get-tuple-element.29.pair_ref, s32[8,128]{1,0:T(8,128)S(1)} %get-tuple-element.30.rank_ref, s32[8,128]{1,0:T(8,128)S(1)} %get-tuple-element.31.table_ref), custom_call_target="tpu_custom_call" | custom-call | tf_op jit(solution)/shard_map/finish/pallas_call | solution.py:303
  (5 shorter events, 0.0 us)
Async XLA Ops:
  4.9 8.2 %collective-permute-start.9 = (bf16[784,128]{1,0:T(8,128)(2,1)S(1)}, bf16[784,128]{1,0:T(8,128)(2,1)S(1)}, u32[]{:S(2)}, u32[]{:S(2)}) collective-permute-start(bf16[784,128]{1,0:T(8,128)(2,1)S(1)} %get-tuple-element.23.refs_2_), channel_id=1, source_target_pairs={{0,1},{1,0},{2,3},{3,2},{4,5},{5,4},{6,7},{7,6},{8,9},{9,8},{10,11... | collective-permute-start | bytes 602120 | tf_op jit(solution)/shard_map/ppermute | solution.py:348
  5.5 10.6 %collective-permute-start = (bf16[784,128]{1,0:T(8,128)(2,1)S(1)}, bf16[784,128]{1,0:T(8,128)(2,1)S(1)}, u32[]{:S(2)}, u32[]{:S(2)}) collective-permute-start(bf16[784,128]{1,0:T(8,128)(2,1)S(1)} %get-tuple-element.18), channel_id=1, source_target_pairs={{0,12},{1,13},{2,14},{3,15},{4,8},{5,9},{6,10},{7,11},{8,4},{9,5},... | collective-permute-start | bytes 602120 | tf_op jit(solution)/shard_map/ppermute | solution.py:343
  10.2 15.5 %collective-permute-start.1 = (bf16[784,128]{1,0:T(8,128)(2,1)S(1)}, bf16[784,128]{1,0:T(8,128)(2,1)S(1)}, u32[]{:S(2)}, u32[]{:S(2)}) collective-permute-start(bf16[784,128]{1,0:T(8,128)(2,1)S(1)} %get-tuple-element.19), channel_id=1, source_target_pairs={{0,14},{1,15},{2,12},{3,13},{4,10},{5,11},{6,8},{7,9},{8,6},{9,7},... | collective-permute-start | bytes 602120 | tf_op jit(solution)/shard_map/ppermute | solution.py:343
  11.3 22.6 %collective-permute-start.2 = (bf16[784,128]{1,0:T(8,128)(2,1)S(1)}, bf16[784,128]{1,0:T(8,128)(2,1)S(1)}, u32[]{:S(2)}, u32[]{:S(2)}) collective-permute-start(bf16[784,128]{1,0:T(8,128)(2,1)S(1)} %get-tuple-element.24), channel_id=1, source_target_pairs={{0,4},{1,5},{2,6},{3,7},{4,0},{5,1},{6,2},{7,3},{8,12},{9,13},{10,... | collective-permute-start | bytes 602120 | tf_op jit(solution)/shard_map/ppermute | solution.py:343
  11.3 22.6 %collective-permute-start.3 = (bf16[784,128]{1,0:T(8,128)(2,1)S(1)}, bf16[784,128]{1,0:T(8,128)(2,1)S(1)}, u32[]{:S(2)}, u32[]{:S(2)}) collective-permute-start(bf16[784,128]{1,0:T(8,128)(2,1)S(1)} %get-tuple-element.25), channel_id=1, source_target_pairs={{0,6},{1,7},{2,4},{3,5},{4,2},{5,3},{6,0},{7,1},{8,14},{9,15},{10,... | collective-permute-start | bytes 602120 | tf_op jit(solution)/shard_map/ppermute | solution.py:343
  13.2 21.3 %collective-permute-start.4 = (bf16[784,128]{1,0:T(8,128)(2,1)S(1)}, bf16[784,128]{1,0:T(8,128)(2,1)S(1)}, u32[]{:S(2)}, u32[]{:S(2)}) collective-permute-start(bf16[784,128]{1,0:T(8,128)(2,1)S(1)} %get-tuple-element.26), channel_id=1, source_target_pairs={{0,2},{1,3},{2,0},{3,1},{4,6},{5,7},{6,4},{7,5},{8,10},{9,11},{10,... | collective-permute-start | bytes 602120 | tf_op jit(solution)/shard_map/ppermute | solution.py:343
  16.1 26.0 %collective-permute-start.5 = (bf16[784,128]{1,0:T(8,128)(2,1)S(1)}, bf16[784,128]{1,0:T(8,128)(2,1)S(1)}, u32[]{:S(2)}, u32[]{:S(2)}) collective-permute-start(bf16[784,128]{1,0:T(8,128)(2,1)S(1)} %get-tuple-element.27), channel_id=1, source_target_pairs={{0,8},{1,9},{2,10},{3,11},{4,12},{5,13},{6,14},{7,15},{8,0},{9,1},... | collective-permute-start | bytes 602120 | tf_op jit(solution)/shard_map/ppermute | solution.py:343
  25.6 21.2 %collective-permute-start.6 = (bf16[784,128]{1,0:T(8,128)(2,1)S(1)}, bf16[784,128]{1,0:T(8,128)(2,1)S(1)}, u32[]{:S(2)}, u32[]{:S(2)}) collective-permute-start(bf16[784,128]{1,0:T(8,128)(2,1)S(1)} %get-tuple-element.28), channel_id=1, source_target_pairs={{0,10},{1,11},{2,8},{3,9},{4,14},{5,15},{6,12},{7,13},{8,2},{9,3},... | collective-permute-start | bytes 602120 | tf_op jit(solution)/shard_map/ppermute | solution.py:343
  34.0 12.9 %collective-permute-start.7 = (bf16[784,128]{1,0:T(8,128)(2,1)S(1)}, bf16[784,128]{1,0:T(8,128)(2,1)S(1)}, u32[]{:S(2)}, u32[]{:S(2)}) collective-permute-start(bf16[784,128]{1,0:T(8,128)(2,1)S(1)} %collective-permute-done.refs_0_), channel_id=1, source_target_pairs={{0,1},{1,0},{2,3},{3,2},{4,5},{5,4},{6,7},{7,6},{8,9},{9,8},{10,11... | collective-permute-start | bytes 602120 | tf_op jit(solution)/shard_map/ppermute | solution.py:348
  34.0 13.4 %collective-permute-start.8 = (bf16[784,128]{1,0:T(8,128)(2,1)S(1)}, bf16[784,128]{1,0:T(8,128)(2,1)S(1)}, u32[]{:S(2)}, u32[]{:S(2)}) collective-permute-start(bf16[784,128]{1,0:T(8,128)(2,1)S(1)} %collective-permute-done.1.refs_1_), channel_id=1, source_target_pairs={{0,1},{1,0},{2,3},{3,2},{4,5},{5,4},{6,7},{7,6},{8,9},{9,8},{10,11... | collective-permute-start | bytes 602120 | tf_op jit(solution)/shard_map/ppermute | solution.py:348
  34.5 13.8 %collective-permute-start.10 = (bf16[784,128]{1,0:T(8,128)(2,1)S(1)}, bf16[784,128]{1,0:T(8,128)(2,1)S(1)}, u32[]{:S(2)}, u32[]{:S(2)}) collective-permute-start(bf16[784,128]{1,0:T(8,128)(2,1)S(1)} %collective-permute-done.2.refs_3_), channel_id=1, source_target_pairs={{0,1},{1,0},{2,3},{3,2},{4,5},{5,4},{6,7},{7,6},{8,9},{9,8},{10,11... | collective-permute-start | bytes 602120 | tf_op jit(solution)/shard_map/ppermute | solution.py:348
  42.1 6.2 %collective-permute-start.11 = (bf16[784,128]{1,0:T(8,128)(2,1)S(1)}, bf16[784,128]{1,0:T(8,128)(2,1)S(1)}, u32[]{:S(2)}, u32[]{:S(2)}) collective-permute-start(bf16[784,128]{1,0:T(8,128)(2,1)S(1)} %collective-permute-done.3.refs_4_), channel_id=1, source_target_pairs={{0,1},{1,0},{2,3},{3,2},{4,5},{5,4},{6,7},{7,6},{8,9},{9,8},{10,11... | collective-permute-start | bytes 602120 | tf_op jit(solution)/shard_map/ppermute | solution.py:348
  46.8 1.4 %collective-permute-start.12 = (bf16[784,128]{1,0:T(8,128)(2,1)S(1)}, bf16[784,128]{1,0:T(8,128)(2,1)S(1)}, u32[]{:S(2)}, u32[]{:S(2)}) collective-permute-start(bf16[784,128]{1,0:T(8,128)(2,1)S(1)} %collective-permute-done.4.refs_5_), channel_id=1, source_target_pairs={{0,1},{1,0},{2,3},{3,2},{4,5},{5,4},{6,7},{7,6},{8,9},{9,8},{10,11... | collective-permute-start | bytes 602120 | tf_op jit(solution)/shard_map/ppermute | solution.py:348
  46.8 3.7 %collective-permute-start.13 = (bf16[784,128]{1,0:T(8,128)(2,1)S(1)}, bf16[784,128]{1,0:T(8,128)(2,1)S(1)}, u32[]{:S(2)}, u32[]{:S(2)}) collective-permute-start(bf16[784,128]{1,0:T(8,128)(2,1)S(1)} %collective-permute-done.5.refs_6_), channel_id=1, source_target_pairs={{0,1},{1,0},{2,3},{3,2},{4,5},{5,4},{6,7},{7,6},{8,9},{9,8},{10,11... | collective-permute-start | bytes 602120 | tf_op jit(solution)/shard_map/ppermute | solution.py:348
  47.3 3.2 %collective-permute-start.14 = (bf16[784,128]{1,0:T(8,128)(2,1)S(1)}, bf16[784,128]{1,0:T(8,128)(2,1)S(1)}, u32[]{:S(2)}, u32[]{:S(2)}) collective-permute-start(bf16[784,128]{1,0:T(8,128)(2,1)S(1)} %collective-permute-done.6.refs_7_), channel_id=1, source_target_pairs={{0,1},{1,0},{2,3},{3,2},{4,5},{5,4},{6,7},{7,6},{8,9},{9,8},{10,11... | collective-permute-start | bytes 602120 | tf_op jit(solution)/shard_map/ppermute | solution.py:348
where the time goes:
time: 65.4 us; the launch traced here: 65.2 us
  starting transfers between devices  28.9 us (44%)
  waiting for transfers between devices  13.6 us (21%)
  blocking collectives  12 us (18%)
  Pallas kernels  10 us (15%)
  between operations  0.71 us (1%)
    ppermute x7, starting transfers between devices, body(): lax.ppermute(own[m], 'owner', [(d, d ^ 2 * m) for d in range(owners)])  27.2 us
    ppermute x7, waiting for transfers between devices, body(): lax.ppermute(own[m], 'owner', [(d, d ^ 2 * m) for d in range(owners)])  13.5 us
    all_to_all x1, blocking collectives, body(): lax.all_to_all(best, 'owner', split_axis=0, concat_axis=0, tiled=True)  12 us
    pallas_call x3, Pallas kernels, stage(): pl.pallas_call(functools.partial(stage_kernel, old=old, new=total - old,...  5 us
    pallas_call x1, Pallas kernels, first_blocks(): pl.pallas_call(functools.partial(first_kernel, numbers=numbers, pairs=pai...  2.3 us
    pallas_call x1, Pallas kernels, later_blocks(): pl.pallas_call(functools.partial(later_kernel, numbers=numbers, capacity=...  1.98 us
    ppermute x8, starting transfers between devices, body(): other[m] = lax.ppermute(own[m], 'owner', swap)  1.72 us
  transfers between devices with their start and end apart: 15, of which 3 were waited for; matrix products, arithmetic and copies ran while one was open for 0% of the time, Pallas kernels for 5%

commit v1 on v0

--- a/solution.py
+++ b/solution.py
@@ -9,7 +9,7 @@
 
 
 LANES = 128
-EXTRA = 16
+EXTRA = 8
 F32 = jnp.float32
 BF16 = jnp.bfloat16
 VMEM = pl.BlockSpec(memory_space=pltpu.VMEM)
@@ -82,7 +82,7 @@
     width = rows.shape[1]
     slabs = width // LANES
     label = jnp.concatenate([label_ref[k : k + 1, :] for k in range(chunks)], axis=1)
-    label = jnp.broadcast_to(label, (EXTRA, chunks * LANES)).astype(BF16)
+    label = jnp.broadcast_to(label, (16, chunks * LANES)).astype(BF16)
     place = iota((capacity, LANES), 0).astype(F32)
     for block, m in zip(blocks, numbers):
         chosen = jnp.concatenate(
@@ -100,7 +100,7 @@
         )
         for k in range(slabs):
             block[k * capacity : (k + 1) * capacity, :] = unit[:, k * LANES : (k + 1) * LANES]
-        block[slabs * capacity : slabs * capacity + EXTRA, 0:capacity] = labels.astype(BF16)
+        block[slabs * capacity : slabs * capacity + EXTRA, 0:capacity] = labels.astype(BF16)[0:EXTRA, :]
 
 
 def first_kernel(ids_hbm, owners_hbm, rows_hbm, *refs, numbers, pairs, capacity, clusters):
@@ -168,63 +168,74 @@
     )(near(slot), near(label), near(rows))
 
 
-def stage_kernel(*refs, old, new, capacity, width, last):
-    slabs = width // LANES
-    group = LANES // capacity
-    total = old + new
+def span(first, stop):
+    return slice(first * LANES, stop * LANES)
+
+
+def place(block, keys, marks, at, capacity):
+    slabs = keys.shape[1] // LANES
+    for k in range(slabs):
+        keys[at : at + capacity, k * LANES : (k + 1) * LANES] = block[
+            k * capacity : (k + 1) * capacity, :
+        ]
+    marks[0:1, at : at + capacity] = block[
+        slabs * capacity : slabs * capacity + EXTRA, 0:capacity
+    ].astype(F32)[0:1, :]
+
+
+def stage_kernel(*refs, own, other, fresh, items, capacity, last):
     refs = list(refs)
-    blocks = [refs.pop(0) for _ in range(2 * total)]
-    best_in = refs.pop(0) if old else None
-    out_ref, keys, marks = refs
-    for b, block in enumerate(blocks):
-        at = b * capacity
-        for k in range(slabs):
-            keys[at : at + capacity, k * LANES : (k + 1) * LANES] = block[
-                k * capacity : (k + 1) * capacity, :
-            ]
-        marks[0:1, at : at + capacity] = block[
-            slabs * capacity : slabs * capacity + EXTRA, 0:capacity
-        ].astype(F32)[0:1, :]
-    tiles, old_tiles = total // group, old // group
-    best = [best_in[:, t * LANES : (t + 1) * LANES] for t in range(old_tiles)]
-    best += [jnp.full((8, LANES), -1.0, F32)] * (tiles - old_tiles)
-
-    def span(first, stop):
-        return slice(first * LANES, stop * LANES)
-
-    def visit(key_first, key_stop, first, stop):
-        for left in range(key_first, key_stop, 2):
-            right = min(left + 2, key_stop)
+    blocks = [refs.pop(0) for _ in range(own[1] - own[0] + other[1] - other[0])]
+    if not fresh:
+        refs = refs[3:]
+    keys, marks, state = refs[:3]
+    starts = [b * capacity for b in range(*own)] + [items + b * capacity for b in range(*other)]
+    for block, at in zip(blocks, starts):
+        place(block, keys, marks, at, capacity)
+    group, tiles = LANES // capacity, items // LANES
+    old, total = (n // group for n in own)
+    old_other, total_other = (tiles + n // group for n in other)
+    best = {t: state[:, span(t, t + 1)] for t in range(old)}
+    best |= {t: jnp.full((8, LANES), -1.0, F32) for t in range(old, total)}
+
+    def meet(left, right, first, stop):
+        if first == stop:
+            return
+        for low in range(left, right, 2):
+            high = min(low + 2, right)
             gram = lax.dot_general(
-                keys[span(left, right), :],
+                keys[span(low, high), :],
                 keys[span(first, stop), :],
                 (((1,), (1,)), ((), ())),
                 preferred_element_type=F32,
             )
-            for key in range(left, right):
+            for key in range(low, high):
                 column = jnp.broadcast_to(marks[0:1, span(key, key + 1)], (LANES, LANES)).T
                 for t in range(first, stop):
                     same = column == marks[0:1, span(t, t + 1)]
                     if t == key:
                         same = same & (iota((LANES, LANES), 0) != iota((LANES, LANES), 1))
-                    piece = gram[span(key - left, key - left + 1), span(t - first, t - first + 1)]
+                    piece = gram[span(key - low, key - low + 1), span(t - first, t - first + 1)]
                     piece = jnp.where(same, piece, -1.0)
                     top = jnp.max(piece.reshape(LANES // 8, 8, LANES), axis=0)
                     best[t] = jnp.maximum(best[t], top)
 
-    visit(0, 2 * tiles, old_tiles, tiles)
-    if old:
-        visit(old_tiles, tiles, 0, old_tiles)
-        visit(tiles + old_tiles, 2 * tiles, 0, old_tiles)
+    meet(0, total, old, total)
+    meet(tiles, total_other, old, total)
+    meet(old, total, 0, old)
+    meet(old_other, total_other, 0, old)
     if last is None:
-        for t in range(tiles):
-            out_ref[:, span(t, t + 1)] = best[t]
-        return
-    numbers, per_pair = last
-    pairs = len(numbers)
+        for t in range(total):
+            state[:, span(t, t + 1)] = best[t]
+    else:
+        settle(best, marks, refs[3], capacity, **last)
+
+
+def settle(best, marks, out_ref, capacity, numbers, per_pair):
+    pairs, tiles = len(numbers), len(best)
     owner = lax.axis_index("owner")
     chip, core = owner // 2, owner % 2
-    rows = [jnp.max(b, axis=0, keepdims=True) for b in best]
+    rows = [jnp.max(best[t], axis=0, keepdims=True) for t in range(tiles)]
     row = jnp.concatenate(rows, axis=0)
     mark = jnp.concatenate([marks[0:1, span(t, t + 1)] for t in range(tiles)], axis=0)
     sums, counts = [], []
@@ -233,43 +244,45 @@
         sums.append(jnp.sum(jnp.where(mine, row, 0.0), axis=0, keepdims=True))
         counts.append(jnp.sum(mine.astype(F32), axis=0, keepdims=True))
     stats = jnp.sum(jnp.concatenate(sums + counts, axis=0), axis=1, keepdims=True)
-    stats = jnp.concatenate(
-        [
-            jnp.broadcast_to(stats, (2 * per_pair, LANES)),
-            jnp.zeros((LANES - 2 * per_pair, LANES), F32),
-        ],
-        axis=0,
-    ).T[0:1, :]
-    for d in range(2 * pairs):
-        out_ref[d, 1:2, :] = stats
-    for t in range(tiles):
-        marks[1:2, span(t, t + 1)] = rows[t]
+    stats = jnp.where(iota((2 * per_pair, LANES), 0) == iota((2 * per_pair, LANES), 1), stats, 0.0)
+    stats = jnp.sum(stats, axis=0, keepdims=True)
+    out_ref[:, span(1, 2)] = jnp.broadcast_to(stats, (2 * pairs, LANES))
+    target = iota((2 * pairs, LANES), 0)
+    back = jnp.zeros((2 * pairs, LANES), F32)
     for b, m in enumerate(numbers):
-        out_ref[2 * (chip ^ m) + core, 0:1, 0:capacity] = marks[
-            1:2, b * capacity : (b + 1) * capacity
-        ]
-
-
-def stage(own, other, old, best, width, capacity, last):
-    total = len(own)
-    if last is None:
-        out = pltpu.VMEM((8, total * capacity), F32)
-    else:
-        out = jax.ShapeDtypeStruct((2 * total, 8, LANES), F32)
-    args = [near(b) for b in own] + [near(b) for b in other]
-    if old:
-        args.append(near(best))
+        line, shift = rows[b * capacity // LANES], b * capacity % LANES
+        if shift:
+            line = pltpu.roll(jnp.broadcast_to(line, (8, LANES)), LANES - shift, 1)[0:1, :]
+        back = jnp.where(target == 2 * (chip ^ m) + core, line, back)
+    out_ref[:, span(0, 1)] = back
+
+
+def stage(new_own, new_other, own, other, state, items, width, capacity, last):
+    args = [near(b) for b in new_own + new_other]
+    fresh = state is None
+    out = [
+        pltpu.VMEM((2 * items, width), BF16),
+        pltpu.VMEM((8, 2 * items), F32),
+        pltpu.VMEM((8, items), F32),
+    ]
+    aliases = {} if fresh else {len(args) + k: k for k in range(3)}
+    args += [] if fresh else [near(a) for a in state]
+    if last is not None:
+        out.append(pltpu.VMEM((2 * len(last["numbers"]), 2 * LANES), F32))
     return pl.pallas_call(
         functools.partial(
-            stage_kernel, old=old, new=total - old, capacity=capacity, width=width, last=last
+            stage_kernel,
+            own=own,
+            other=other,
+            fresh=fresh,
+            items=items,
+            capacity=capacity,
+            last=last,
         ),
         in_specs=[VMEM] * len(args),
-        out_specs=VMEM,
+        out_specs=[VMEM] * len(out),
         out_shape=out,
-        scratch_shapes=[
-            pltpu.VMEM((2 * total * capacity, width), BF16),
-            pltpu.VMEM((8, 2 * total * capacity), F32),
-        ],
+        input_output_aliases=aliases,
         name="stage",
         compiler_params=PARAMS,
     )(*args)
@@ -284,9 +297,10 @@
     total = jnp.zeros((1, padded), F32)
     number = jnp.zeros((1, padded), F32)
     for p in range(pairs):
-        got = lane_take(back_ref[2 * p + core, 0:1, :], rank)
+        got = jnp.where(core == 0, back_ref[2 * p : 2 * p + 1, span(0, 1)], back_ref[2 * p + 1 : 2 * p + 2, span(0, 1)])
+        got = lane_take(got, rank)
         maxima = jnp.where(pair == p, got, maxima)
-        stats = back_ref[2 * p, 1:2, :] + back_ref[2 * p + 1, 1:2, :]
+        stats = back_ref[2 * p : 2 * p + 1, span(1, 2)] + back_ref[2 * p + 1 : 2 * p + 2, span(1, 2)]
         mine = pair_row == p
         index = jnp.where(mine, local_row, 0)
         parts = [index[:, f : f + LANES] for f in range(0, padded, LANES)]
@@ -310,15 +324,15 @@
         ],
         name="finish",
         compiler_params=PARAMS,
-    )(back, near(pair), near(rank), near(table))
+    )(near(back), near(pair), near(rank), near(table))
 
 
 def plan(pairs):
-    quarter = pairs // 4
-    parts = [list(range(hi * quarter, (hi + 1) * quarter)) for hi in range(4)]
-    sent = parts[3] + parts[2] + parts[1] + parts[0]
-    stages = [parts[3] + parts[0][:1], parts[1] + parts[0][1:], parts[2]]
-    return sent, quarter, stages
+    size = pairs // 8
+    part = [list(range(k * size, (k + 1) * size)) for k in range(8)]
+    sent = part[6] + part[7] + part[4] + part[5] + part[2] + part[3] + part[1] + part[0]
+    stages = [part[0] + part[6] + part[2], part[3] + part[1], part[7], part[4], part[5]]
+    return sent, 2 * size, stages, part[0]
 
 
 def body(embeddings, cluster_ids, owner_map):
@@ -329,36 +343,41 @@
     capacity = items // pairs
     per_pair = clusters // pairs
     ids = cluster_ids.reshape(items // LANES, LANES)
-    sent, head, stages = plan(pairs)
+    sent, head, stages, local = plan(pairs)
     *blocks, pair, rank, label, table, slot, rows = first_blocks(
         ids, owner_map.reshape(1, clusters), embeddings, sent[:head], pairs, capacity
     )
     blocks += later_blocks(slot, label, rows, sent[head:], capacity)
     blocks = dict(zip(sent, blocks))
     swap = [(d, d ^ 1) for d in range(owners)]
-    own = {}
+    own, other = {}, {}
     for m in sent:
         own[m] = blocks[m]
         if m:
             own[m] = lax.ppermute(own[m], "owner", [(d, d ^ (2 * m)) for d in range(owners)])
-    other = {}
-    done, best = [], None
-    for index, new in enumerate(stages):
-        for m in new:
-            other[m] = lax.ppermute(own[m], "owner", swap)
-        numbers = done + new
-        last = (tuple(numbers), per_pair) if index == len(stages) - 1 else None
-        best = stage(
-            [own[m] for m in numbers],
-            [other[m] for m in numbers],
-            len(done),
-            best,
+    order = tuple(m for new in stages for m in new)
+    for m in order:
+        other[m] = lax.ppermute(own[m], "owner", swap)
+    state, mine, theirs = None, 0, 0
+    waiting = local
+    for new in stages + [[]]:
+        last = None if new else dict(numbers=order, per_pair=per_pair)
+        own_range, other_range = (mine, mine + len(new)), (theirs, theirs + len(waiting))
+        result = stage(
+            [own[m] for m in new],
+            [other[m] for m in waiting],
+            own_range,
+            other_range,
+            state,
+            items,
             width,
             capacity,
             last,
         )
-        done = numbers
-    back = lax.all_to_all(best, "owner", split_axis=0, concat_axis=0, tiled=True)
+        state = result[:3]
+        mine, theirs = own_range[1], other_range[1]
+        waiting = list(order[theirs:mine])
+    back = lax.all_to_all(result[3], "owner", split_axis=0, concat_axis=0, tiled=True)
     maxima, mean = finish(back, pair, rank, table, clusters, pairs, per_pair)
     return maxima.reshape(items), mean.reshape(clusters)
 

time: 65.4 us -> 66.2 us (1.012)
  waiting for transfers between devices: 13.6 us -> 21.9 us
  starting transfers between devices: 28.9 us -> 21.4 us
  blocking collectives: 12 us -> 9.79 us
  Pallas kernels: 10 us -> 12.2 us
    ppermute x7, waiting for transfers between devices: 13.5 us -> 21.8 us  [body(): lax.ppermute(own[m], 'owner', [(d, d ^ 2 * m) for d in range(owners)])]
    ppermute x7, starting transfers between devices: 27.2 us -> 20.3 us  [body(): lax.ppermute(own[m], 'owner', [(d, d ^ 2 * m) for d in range(owners)])]
    all_to_all x1, blocking collectives: 12 us -> 9.79 us  [body(): lax.all_to_all(result[3], 'owner', split_axis=0, concat_axis=0, tiled=True)]
    pallas_call x3 -> x6, Pallas kernels: 5 us -> 7.16 us  [stage(): pl.pallas_call(functools.partial(stage_kernel, own=own, other=other, fres...]
  transfers between devices with their start and end apart: 15 -> 15, of which waited for: 3 -> 4; matrix products, arithmetic and copies ran while one was open for 0% -> 0% of each run, Pallas kernels for 5% -> 10%
where the time goes in v1:
time: 66.2 us; the launch traced here: 66 us
  waiting for transfers between devices  21.9 us (33%)
  starting transfers between devices  21.4 us (32%)
  Pallas kernels  12.2 us (18%)
  blocking collectives  9.79 us (15%)
  between operations  0.75 us (1%)
    ppermute x7, waiting for transfers between devices, body(): lax.ppermute(own[m], 'owner', [(d, d ^ 2 * m) for d in range(owners)])  21.8 us
    ppermute x7, starting transfers between devices, body(): lax.ppermute(own[m], 'owner', [(d, d ^ 2 * m) for d in range(owners)])  20.3 us
    all_to_all x1, blocking collectives, body(): lax.all_to_all(result[3], 'owner', split_axis=0, concat_axis=0, tiled=True)  9.79 us
    pallas_call x6, Pallas kernels, stage(): pl.pallas_call(functools.partial(stage_kernel, own=own, other=other, fres...  7.16 us
    pallas_call x1, Pallas kernels, first_blocks(): pl.pallas_call(functools.partial(first_kernel, numbers=numbers, pairs=pai...  2.3 us
    pallas_call x1, Pallas kernels, later_blocks(): pl.pallas_call(functools.partial(later_kernel, numbers=numbers, capacity=...  1.98 us
  transfers between devices with their start and end apart: 15, of which 4 were waited for; matrix products, arithmetic and copies ran while one was open for 0% of the time, Pallas kernels for 10%

profile of v1, /device:TPU:0, one launch (start us, length us, event | category | flops | bytes accessed | tf_op | source)
XLA Modules:
  0.0 66.0 jit_solution(6861263513460272728)
XLA Ops:
  0.6 2.3 %first.1 = (bf16[776,128]{1,0:T(8,128)(2,1)S(1)}, bf16[776,128]{1,0:T(8,128)(2,1)S(1)}, s32[8,128]{1,0:T(8,128)S(1)}, s32[8,128]{1,0:T(8,128)S(1)}, f32[8,128]{1...) custom-call(s32[8,128]{1,0:T(8,128)} %bitcast.10, s32[1,64]{1,0:T(1,128)} %bitcast.11, ...), custom_call_target="tpu_custom_call" | custom-call | tf_op jit(solution)/shard_map/first/pallas_call | solution.py:129
  2.9 2.0 %later.1 = (bf16[776,128]{1,0:T(8,128)(2,1)S(1)}, bf16[776,128]{1,0:T(8,128)(2,1)S(1)}, bf16[776,128]{1,0:T(8,128)(2,1)S(1)}, bf16[776,128]{1,0:T(8,128)(2,1)S(1...) custom-call(f32[64,128]{1,0:T(8,128)S(1)} %get-tuple-element.34.slot_ref, ...), custom_call_target="tpu_custom_call" | custom-call | tf_op jit(solution)/shard_map/later/pallas_call | solution.py:161
  4.9 3.1 %collective-permute-start.12 = (bf16[776,128]{1,0:T(8,128)(2,1)S(1)}, bf16[776,128]{1,0:T(8,128)(2,1)S(1)}, u32[]{:S(2)}, u32[]{:S(2)}) collective-permute-start(bf16[776,128]{1,0:T(8,128)(2,1)S(1)} %get-tuple-element.43), channel_id=1, source_target_pairs={{0,4},{1,5},{2,6},{3,7},{4,0},{5,1},{6,2},{7,3},{8,12},{9,13},{10,... | collective-permute-start | bytes 595976 | tf_op jit(solution)/shard_map/ppermute | solution.py:357
  8.0 0.0 collective-permute-start.14
  8.0 2.5 %collective-permute-start.10 = (bf16[776,128]{1,0:T(8,128)(2,1)S(1)}, bf16[776,128]{1,0:T(8,128)(2,1)S(1)}, u32[]{:S(2)}, u32[]{:S(2)}) collective-permute-start(bf16[776,128]{1,0:T(8,128)(2,1)S(1)} %get-tuple-element.42), channel_id=1, source_target_pairs={{0,12},{1,13},{2,14},{3,15},{4,8},{5,9},{6,10},{7,11},{8,4},{9,5},... | collective-permute-start | bytes 595976 | tf_op jit(solution)/shard_map/ppermute | solution.py:357
  10.5 1.6 %collective-permute-start.6 = (bf16[776,128]{1,0:T(8,128)(2,1)S(1)}, bf16[776,128]{1,0:T(8,128)(2,1)S(1)}, u32[]{:S(2)}, u32[]{:S(2)}) collective-permute-start(bf16[776,128]{1,0:T(8,128)(2,1)S(1)} %get-tuple-element.40), channel_id=1, source_target_pairs={{0,6},{1,7},{2,4},{3,5},{4,2},{5,3},{6,0},{7,1},{8,14},{9,15},{10,... | collective-permute-start | bytes 595976 | tf_op jit(solution)/shard_map/ppermute | solution.py:357
  12.2 0.5 collective-permute-start.8
  12.7 0.7 %collective-permute-done.12.refs_2_ = bf16[776,128]{1,0:T(8,128)(2,1)S(1)} collective-permute-done((bf16[776,128]{1,0:T(8,128)(2,1)S(1)}, bf16[776,128]{1,0:T(8,128)(2,1)S(1)}, u32[]{:S(2)}, u32[]{:S(2)}) %collective-permute-start.12) | collective-permute-done | bytes 198688 | tf_op jit(solution)/shard_map/ppermute | solution.py:357
  13.3 9.7 %collective-permute-start.4 = (bf16[776,128]{1,0:T(8,128)(2,1)S(1)}, bf16[776,128]{1,0:T(8,128)(2,1)S(1)}, u32[]{:S(2)}, u32[]{:S(2)}) collective-permute-start(bf16[776,128]{1,0:T(8,128)(2,1)S(1)} %get-tuple-element.39), channel_id=1, source_target_pairs={{0,14},{1,15},{2,12},{3,13},{4,10},{5,11},{6,8},{7,9},{8,6},{9,7},... | collective-permute-start | bytes 595976 | tf_op jit(solution)/shard_map/ppermute | solution.py:357
  23.1 0.0 collective-permute-done.14.refs_3_
  23.1 2.9 %collective-permute-start = (bf16[776,128]{1,0:T(8,128)(2,1)S(1)}, bf16[776,128]{1,0:T(8,128)(2,1)S(1)}, u32[]{:S(2)}, u32[]{:S(2)}) collective-permute-start(bf16[776,128]{1,0:T(8,128)(2,1)S(1)} %get-tuple-element.37), channel_id=1, source_target_pairs={{0,10},{1,11},{2,8},{3,9},{4,14},{5,15},{6,12},{7,13},{8,2},{9,3},... | collective-permute-start | bytes 595976 | tf_op jit(solution)/shard_map/ppermute | solution.py:357
  26.0 0.0 collective-permute-done.6.refs_0_
  26.0 0.0 collective-permute-start.13
  26.0 0.0 collective-permute-done.8.refs_1_
  26.0 0.5 collective-permute-start.11
  26.5 3.7 %collective-permute-done.4.refs_0_ = bf16[776,128]{1,0:T(8,128)(2,1)S(1)} collective-permute-done((bf16[776,128]{1,0:T(8,128)(2,1)S(1)}, bf16[776,128]{1,0:T(8,128)(2,1)S(1)}, u32[]{:S(2)}, u32[]{:S(2)}) %collective-permute-start.4) | collective-permute-done | bytes 198688 | tf_op jit(solution)/shard_map/ppermute | solution.py:357
  30.2 0.0 collective-permute-start.7
  30.2 13.2 %collective-permute-done.2.refs_0_ = bf16[776,128]{1,0:T(8,128)(2,1)S(1)} collective-permute-done((bf16[776,128]{1,0:T(8,128)(2,1)S(1)}, bf16[776,128]{1,0:T(8,128)(2,1)S(1)}, u32[]{:S(2)}, u32[]{:S(2)}) %collective-permute-start.2) | collective-permute-done | bytes 198688 | tf_op jit(solution)/shard_map/ppermute | solution.py:357
  43.4 4.2 %collective-permute-done.refs_0_ = bf16[776,128]{1,0:T(8,128)(2,1)S(1)} collective-permute-done((bf16[776,128]{1,0:T(8,128)(2,1)S(1)}, bf16[776,128]{1,0:T(8,128)(2,1)S(1)}, u32[]{:S(2)}, u32[]{:S(2)}) %collective-permute-start) | collective-permute-done | bytes 198688 | tf_op jit(solution)/shard_map/ppermute | solution.py:357
  47.7 0.5 collective-permute-start.3
  48.2 0.1 collective-permute-start.1
  48.2 0.7 %stage.6 = (bf16[2048,768]{1,0:T(8,128)(2,1)S(1)}, f32[8,2048]{1,0:T(8,128)S(1)}, f32[8,1024]{1,0:T(8,128)S(1)}) custom-call(bf16[776,128]{1,0:T(8,128)(2,1)S(1)} %get-tuple-element.44.refs_0_, bf16[776,128]{1,0:T(8,128)(2,1)S(1)} %collective-permute-done.10.refs_1_, bf16[776,128]{1,0:T(8,128)(2,1)S(1)} %collective-permute-done.12.refs_2_, ...), custom_call_target="tpu_custom_call" | custom-call | tf_op jit(solution)/shard_map/stage/pallas_call | solution.py:272
  49.0 1.2 %stage.7 = (bf16[2048,768]{1,0:T(8,128)(2,1)S(1)}, f32[8,2048]{1,0:T(8,128)S(1)}, f32[8,1024]{1,0:T(8,128)S(1)}) custom-call(bf16[776,128]{1,0:T(8,128)(2,1)S(1)} %collective-permute-done.6.refs_0_, bf16[776,128]{1,0:T(8,128)(2,1)S(1)} %collective-permute-done.8.refs_1_, ...), custom_call_target="tpu_custom_call", output_to_operand_aliasing={{0}: (4, {}), {1}: (5, {}), {2}: (6, {})} | custom-call | tf_op jit(solution)/shard_map/stage/pallas_call | solution.py:272
  50.1 0.0 collective-permute-done.7.refs_1_
  50.2 1.4 %stage.8 = (bf16[2048,768]{1,0:T(8,128)(2,1)S(1)}, f32[8,2048]{1,0:T(8,128)S(1)}, f32[8,1024]{1,0:T(8,128)S(1)}) custom-call(bf16[776,128]{1,0:T(8,128)(2,1)S(1)} %collective-permute-done.4.refs_0_, bf16[776,128]{1,0:T(8,128)(2,1)S(1)} %collective-permute-done.7.refs_1_, ...), custom_call_target="tpu_custom_call", output_to_operand_aliasing={{0}: (3, {}), {1}: (4, {}), {2}: (5, {})} | custom-call | tf_op jit(solution)/shard_map/stage/pallas_call | solution.py:272
  51.6 0.0 collective-permute-done.5.refs_1_
  51.6 1.4 %stage.9 = (bf16[2048,768]{1,0:T(8,128)(2,1)S(1)}, f32[8,2048]{1,0:T(8,128)S(1)}, f32[8,1024]{1,0:T(8,128)S(1)}) custom-call(bf16[776,128]{1,0:T(8,128)(2,1)S(1)} %collective-permute-done.2.refs_0_, bf16[776,128]{1,0:T(8,128)(2,1)S(1)} %collective-permute-done.5.refs_1_, ...), custom_call_target="tpu_custom_call", output_to_operand_aliasing={{0}: (2, {}), {1}: (3, {}), {2}: (4, {})} | custom-call | tf_op jit(solution)/shard_map/stage/pallas_call | solution.py:272
  53.0 1.7 %stage.10 = (bf16[2048,768]{1,0:T(8,128)(2,1)S(1)}, f32[8,2048]{1,0:T(8,128)S(1)}, f32[8,1024]{1,0:T(8,128)S(1)}) custom-call(bf16[776,128]{1,0:T(8,128)(2,1)S(1)} %collective-permute-done.refs_0_, bf16[776,128]{1,0:T(8,128)(2,1)S(1)} %collective-permute-done.3.refs_1_, ...), custom_call_target="tpu_custom_call", output_to_operand_aliasing={{0}: (2, {}), {1}: (3, {}), {2}: (4, {})} | custom-call | tf_op jit(solution)/shard_map/stage/pallas_call | solution.py:272
  54.7 0.0 collective-permute-done.1.refs_0_
  54.7 0.8 %stage.11 = (bf16[2048,768]{1,0:T(8,128)(2,1)S(1)}, f32[8,2048]{1,0:T(8,128)S(1)}, f32[8,1024]{1,0:T(8,128)S(1)}, f32[16,256]{1,0:T(8,128)S(1)}) custom-call(bf16[776,128]{1,0:T(8,128)(2,1)S(1)} %collective-permute-done.1.refs_0_, bf16[2048,768]{1,0:T(8,128)(2,1)S(1)} %get-tuple-element.57.refs_1_, ...), custom_call_target="tpu_custom_call", output_to_operand_aliasing={{0}: (1, {}), {1}: (2, {}), {2}: (3, {})} | custom-call | tf_op jit(solution)/shard_map/stage/pallas_call | solution.py:272
  55.5 9.8 %all_to_all.11 = f32[16,1,256]{2,1,0:T(1,128)S(1)} all-to-all(f32[16,1,256]{2,1,0:T(1,128)S(1)} %copy.20), channel_id=1, replica_groups=mesh['parts'=2,'owner'=16] {'owner'}, dimensions={0} | all-to-all | bytes 32768 | tf_op jit(solution)/shard_map/all_to_all | solution.py:380
  65.3 0.7 %finish.1 = (f32[8,128]{1,0:T(8,128)}, f32[1,64]{1,0:T(1,128)}) custom-call(f32[16,256]{1,0:T(8,128)S(1)} %bitcast.8, s32[8,128]{1,0:T(8,128)S(1)} %get-tuple-element.61.pair_ref, s32[8,128]{1,0:T(8,128)S(1)} %get-tuple-element.62.rank_ref, s32[8,128]{1,0:T(8,128)S(1)} %get-tuple-element.63.table_ref), custom_call_target="tpu_custom_call" | custom-call | tf_op jit(solution)/shard_map/finish/pallas_call | solution.py:317
  (10 shorter events, 0.0 us)
Async XLA Ops:
  4.9 8.4 %collective-permute-start.12 = (bf16[776,128]{1,0:T(8,128)(2,1)S(1)}, bf16[776,128]{1,0:T(8,128)(2,1)S(1)}, u32[]{:S(2)}, u32[]{:S(2)}) collective-permute-start(bf16[776,128]{1,0:T(8,128)(2,1)S(1)} %get-tuple-element.43), channel_id=1, source_target_pairs={{0,4},{1,5},{2,6},{3,7},{4,0},{5,1},{6,2},{7,3},{8,12},{9,13},{10,... | collective-permute-start | bytes 595976 | tf_op jit(solution)/shard_map/ppermute | solution.py:357
  8.0 15.1 %collective-permute-start.14 = (bf16[776,128]{1,0:T(8,128)(2,1)S(1)}, bf16[776,128]{1,0:T(8,128)(2,1)S(1)}, u32[]{:S(2)}, u32[]{:S(2)}) collective-permute-start(bf16[776,128]{1,0:T(8,128)(2,1)S(1)} %get-tuple-element.44.refs_0_), channel_id=1, source_target_pairs={{0,1},{1,0},{2,3},{3,2},{4,5},{5,4},{6,7},{7,6},{8,9},{9,8},{10,11... | collective-permute-start | bytes 595976 | tf_op jit(solution)/shard_map/ppermute | solution.py:360
  8.0 15.1 %collective-permute-start.10 = (bf16[776,128]{1,0:T(8,128)(2,1)S(1)}, bf16[776,128]{1,0:T(8,128)(2,1)S(1)}, u32[]{:S(2)}, u32[]{:S(2)}) collective-permute-start(bf16[776,128]{1,0:T(8,128)(2,1)S(1)} %get-tuple-element.42), channel_id=1, source_target_pairs={{0,12},{1,13},{2,14},{3,15},{4,8},{5,9},{6,10},{7,11},{8,4},{9,5},... | collective-permute-start | bytes 595976 | tf_op jit(solution)/shard_map/ppermute | solution.py:357
  10.5 15.5 %collective-permute-start.6 = (bf16[776,128]{1,0:T(8,128)(2,1)S(1)}, bf16[776,128]{1,0:T(8,128)(2,1)S(1)}, u32[]{:S(2)}, u32[]{:S(2)}) collective-permute-start(bf16[776,128]{1,0:T(8,128)(2,1)S(1)} %get-tuple-element.40), channel_id=1, source_target_pairs={{0,6},{1,7},{2,4},{3,5},{4,2},{5,3},{6,0},{7,1},{8,14},{9,15},{10,... | collective-permute-start | bytes 595976 | tf_op jit(solution)/shard_map/ppermute | solution.py:357
  12.2 13.8 %collective-permute-start.8 = (bf16[776,128]{1,0:T(8,128)(2,1)S(1)}, bf16[776,128]{1,0:T(8,128)(2,1)S(1)}, u32[]{:S(2)}, u32[]{:S(2)}) collective-permute-start(bf16[776,128]{1,0:T(8,128)(2,1)S(1)} %get-tuple-element.41), channel_id=1, source_target_pairs={{0,2},{1,3},{2,0},{3,1},{4,6},{5,7},{6,4},{7,5},{8,10},{9,11},{10,... | collective-permute-start | bytes 595976 | tf_op jit(solution)/shard_map/ppermute | solution.py:357
  13.3 16.9 %collective-permute-start.4 = (bf16[776,128]{1,0:T(8,128)(2,1)S(1)}, bf16[776,128]{1,0:T(8,128)(2,1)S(1)}, u32[]{:S(2)}, u32[]{:S(2)}) collective-permute-start(bf16[776,128]{1,0:T(8,128)(2,1)S(1)} %get-tuple-element.39), channel_id=1, source_target_pairs={{0,14},{1,15},{2,12},{3,13},{4,10},{5,11},{6,8},{7,9},{8,6},{9,7},... | collective-permute-start | bytes 595976 | tf_op jit(solution)/shard_map/ppermute | solution.py:357
  23.1 20.3 %collective-permute-start.2 = (bf16[776,128]{1,0:T(8,128)(2,1)S(1)}, bf16[776,128]{1,0:T(8,128)(2,1)S(1)}, u32[]{:S(2)}, u32[]{:S(2)}) collective-permute-start(bf16[776,128]{1,0:T(8,128)(2,1)S(1)} %get-tuple-element.38), channel_id=1, source_target_pairs={{0,8},{1,9},{2,10},{3,11},{4,12},{5,13},{6,14},{7,15},{8,0},{9,1},... | collective-permute-start | bytes 595976 | tf_op jit(solution)/shard_map/ppermute | solution.py:357
  23.1 24.5 %collective-permute-start = (bf16[776,128]{1,0:T(8,128)(2,1)S(1)}, bf16[776,128]{1,0:T(8,128)(2,1)S(1)}, u32[]{:S(2)}, u32[]{:S(2)}) collective-permute-start(bf16[776,128]{1,0:T(8,128)(2,1)S(1)} %get-tuple-element.37), channel_id=1, source_target_pairs={{0,10},{1,11},{2,8},{3,9},{4,14},{5,15},{6,12},{7,13},{8,2},{9,3},... | collective-permute-start | bytes 595976 | tf_op jit(solution)/shard_map/ppermute | solution.py:357
  26.0 21.7 %collective-permute-start.13 = (bf16[776,128]{1,0:T(8,128)(2,1)S(1)}, bf16[776,128]{1,0:T(8,128)(2,1)S(1)}, u32[]{:S(2)}, u32[]{:S(2)}) collective-permute-start(bf16[776,128]{1,0:T(8,128)(2,1)S(1)} %collective-permute-done.12.refs_2_), channel_id=1, source_target_pairs={{0,1},{1,0},{2,3},{3,2},{4,5},{5,4},{6,7},{7,6},{8,9},{9,8},{10,11... | collective-permute-start | bytes 595976 | tf_op jit(solution)/shard_map/ppermute | solution.py:360
  26.0 22.2 %collective-permute-start.11 = (bf16[776,128]{1,0:T(8,128)(2,1)S(1)}, bf16[776,128]{1,0:T(8,128)(2,1)S(1)}, u32[]{:S(2)}, u32[]{:S(2)}) collective-permute-start(bf16[776,128]{1,0:T(8,128)(2,1)S(1)} %collective-permute-done.10.refs_1_), channel_id=1, source_target_pairs={{0,1},{1,0},{2,3},{3,2},{4,5},{5,4},{6,7},{7,6},{8,9},{9,8},{10,11... | collective-permute-start | bytes 595976 | tf_op jit(solution)/shard_map/ppermute | solution.py:360
  30.2 19.9 %collective-permute-start.7 = (bf16[776,128]{1,0:T(8,128)(2,1)S(1)}, bf16[776,128]{1,0:T(8,128)(2,1)S(1)}, u32[]{:S(2)}, u32[]{:S(2)}) collective-permute-start(bf16[776,128]{1,0:T(8,128)(2,1)S(1)} %collective-permute-done.6.refs_0_), channel_id=1, source_target_pairs={{0,1},{1,0},{2,3},{3,2},{4,5},{5,4},{6,7},{7,6},{8,9},{9,8},{10,11... | collective-permute-start | bytes 595976 | tf_op jit(solution)/shard_map/ppermute | solution.py:360
  43.4 6.7 %collective-permute-start.9 = (bf16[776,128]{1,0:T(8,128)(2,1)S(1)}, bf16[776,128]{1,0:T(8,128)(2,1)S(1)}, u32[]{:S(2)}, u32[]{:S(2)}) collective-permute-start(bf16[776,128]{1,0:T(8,128)(2,1)S(1)} %collective-permute-done.8.refs_1_), channel_id=1, source_target_pairs={{0,1},{1,0},{2,3},{3,2},{4,5},{5,4},{6,7},{7,6},{8,9},{9,8},{10,11... | collective-permute-start | bytes 595976 | tf_op jit(solution)/shard_map/ppermute | solution.py:360
  47.7 3.9 %collective-permute-start.5 = (bf16[776,128]{1,0:T(8,128)(2,1)S(1)}, bf16[776,128]{1,0:T(8,128)(2,1)S(1)}, u32[]{:S(2)}, u32[]{:S(2)}) collective-permute-start(bf16[776,128]{1,0:T(8,128)(2,1)S(1)} %collective-permute-done.4.refs_0_), channel_id=1, source_target_pairs={{0,1},{1,0},{2,3},{3,2},{4,5},{5,4},{6,7},{7,6},{8,9},{9,8},{10,11... | collective-permute-start | bytes 595976 | tf_op jit(solution)/shard_map/ppermute | solution.py:360
  47.7 5.4 %collective-permute-start.3 = (bf16[776,128]{1,0:T(8,128)(2,1)S(1)}, bf16[776,128]{1,0:T(8,128)(2,1)S(1)}, u32[]{:S(2)}, u32[]{:S(2)}) collective-permute-start(bf16[776,128]{1,0:T(8,128)(2,1)S(1)} %collective-permute-done.2.refs_0_), channel_id=1, source_target_pairs={{0,1},{1,0},{2,3},{3,2},{4,5},{5,4},{6,7},{7,6},{8,9},{9,8},{10,11... | collective-permute-start | bytes 595976 | tf_op jit(solution)/shard_map/ppermute | solution.py:360
  48.2 6.5 %collective-permute-start.1 = (bf16[776,128]{1,0:T(8,128)(2,1)S(1)}, bf16[776,128]{1,0:T(8,128)(2,1)S(1)}, u32[]{:S(2)}, u32[]{:S(2)}) collective-permute-start(bf16[776,128]{1,0:T(8,128)(2,1)S(1)} %collective-permute-done.refs_0_), channel_id=1, source_target_pairs={{0,1},{1,0},{2,3},{3,2},{4,5},{5,4},{6,7},{7,6},{8,9},{9,8},{10,11... | collective-permute-start | bytes 595976 | tf_op jit(solution)/shard_map/ppermute | solution.py:360

commit v2 on v1

--- a/solution.py
+++ b/solution.py
@@ -10,6 +10,7 @@
 
 LANES = 128
 EXTRA = 8
+CHUNKS = 4
 F32 = jnp.float32
 BF16 = jnp.bfloat16
 VMEM = pl.BlockSpec(memory_space=pltpu.VMEM)
@@ -77,7 +78,7 @@
     rank_ref[...] = item_rank.astype(jnp.int32)
 
 
-def pack(slot_ref, label_ref, rows, blocks, numbers, capacity):
+def pack(slot_ref, label_ref, rows, blocks, numbers, capacity, arrived=None):
     chunks = label_ref.shape[0]
     width = rows.shape[1]
     slabs = width // LANES
@@ -92,7 +93,16 @@
             ],
             axis=1,
         )
-        values = jnp.dot(chosen, rows[...], preferred_element_type=F32)
+        if arrived is None:
+            values = jnp.dot(chosen, rows[...], preferred_element_type=F32)
+        else:
+            values = jnp.zeros((capacity, width), F32)
+            step = rows.shape[0] // len(arrived)
+            for k, copy in enumerate(arrived):
+                if block is blocks[0]:
+                    copy.wait()
+                piece = slice(k * step, (k + 1) * step)
+                values += jnp.dot(chosen[:, piece], rows[piece, :], preferred_element_type=F32)
         scale = lax.rsqrt(jnp.mean(values * values, axis=1, keepdims=True) + 1e-06)
         unit = (values * scale * (1.0 / jnp.sqrt(F32(width)))).astype(BF16)
         labels = lax.dot_general(
@@ -107,19 +117,21 @@
     n = len(numbers)
     blocks = refs[:n]
     pair_ref, rank_ref, label_ref, table_ref, slot_ref, rows, ids_ref, owners_ref, pad, sems = refs[n:]
+    step = rows.shape[0] // CHUNKS
+    copies = [(ids_hbm, ids_ref), (owners_hbm, owners_ref)]
+    for k in range(CHUNKS):
+        piece = pl.ds(k * step, step)
+        copies.append((rows_hbm.at[piece, :], rows.at[piece, :]))
     copies = [
         pltpu.make_async_copy(source, target, sems.at[k])
-        for k, (source, target) in enumerate(
-            ((ids_hbm, ids_ref), (owners_hbm, owners_ref), (rows_hbm, rows))
-        )
+        for k, (source, target) in enumerate(copies)
     ]
     for copy in copies:
         copy.start()
     copies[0].wait()
     copies[1].wait()
     route(ids_ref, owners_ref, pair_ref, rank_ref, label_ref, table_ref, slot_ref, pad, pairs, clusters)
-    copies[2].wait()
-    pack(slot_ref, label_ref, rows, blocks, numbers, capacity)
+    pack(slot_ref, label_ref, rows, blocks, numbers, capacity, copies[2:])
 
 
 def first_blocks(ids, owners, rows, numbers, pairs, capacity):
@@ -145,7 +157,7 @@
             pltpu.VMEM(ids.shape, jnp.int32),
             pltpu.VMEM(owners.shape, jnp.int32),
             pltpu.VMEM((8, padded), jnp.int32),
-            pltpu.SemaphoreType.DMA((3,)),
+            pltpu.SemaphoreType.DMA((2 + CHUNKS,)),
         ],
         name="first",
         compiler_params=PARAMS,
@@ -187,22 +199,25 @@
     refs = list(refs)
     blocks = [refs.pop(0) for _ in range(own[1] - own[0] + other[1] - other[0])]
     if not fresh:
-        refs = refs[3:]
-    keys, marks, state = refs[:3]
+        refs = refs[4:]
+    keys, marks, columns, state = refs[:4]
     starts = [b * capacity for b in range(*own)] + [items + b * capacity for b in range(*other)]
     for block, at in zip(blocks, starts):
         place(block, keys, marks, at, capacity)
     group, tiles = LANES // capacity, items // LANES
     old, total = (n // group for n in own)
     old_other, total_other = (tiles + n // group for n in other)
+    for t in [*range(old, total), *range(old_other, total_other)]:
+        columns[span(t, t + 1), :] = jnp.broadcast_to(marks[0:1, span(t, t + 1)], (LANES, LANES)).T
     best = {t: state[:, span(t, t + 1)] for t in range(old)}
     best |= {t: jnp.full((8, LANES), -1.0, F32) for t in range(old, total)}
 
     def meet(left, right, first, stop):
         if first == stop:
             return
-        for low in range(left, right, 2):
-            high = min(low + 2, right)
+        step = max(2, 8 // (stop - first))
+        for low in range(left, right, step):
+            high = min(low + step, right)
             gram = lax.dot_general(
                 keys[span(low, high), :],
                 keys[span(first, stop), :],
@@ -210,7 +225,7 @@
                 preferred_element_type=F32,
             )
             for key in range(low, high):
-                column = jnp.broadcast_to(marks[0:1, span(key, key + 1)], (LANES, LANES)).T
+                column = columns[span(key, key + 1), :]
                 for t in range(first, stop):
                     same = column == marks[0:1, span(t, t + 1)]
                     if t == key:
@@ -228,7 +243,7 @@
         for t in range(total):
             state[:, span(t, t + 1)] = best[t]
     else:
-        settle(best, marks, refs[3], capacity, **last)
+        settle(best, marks, refs[4], capacity, **last)
 
 
 def settle(best, marks, out_ref, capacity, numbers, per_pair):
@@ -263,9 +278,10 @@
     out = [
         pltpu.VMEM((2 * items, width), BF16),
         pltpu.VMEM((8, 2 * items), F32),
+        pltpu.VMEM((2 * items, LANES), F32),
         pltpu.VMEM((8, items), F32),
     ]
-    aliases = {} if fresh else {len(args) + k: k for k in range(3)}
+    aliases = {} if fresh else {len(args) + k: k for k in range(len(out))}
     args += [] if fresh else [near(a) for a in state]
     if last is not None:
         out.append(pltpu.VMEM((2 * len(last["numbers"]), 2 * LANES), F32))
@@ -331,8 +347,16 @@
     size = pairs // 8
     part = [list(range(k * size, (k + 1) * size)) for k in range(8)]
     sent = part[6] + part[7] + part[4] + part[5] + part[2] + part[3] + part[1] + part[0]
-    stages = [part[0] + part[6] + part[2], part[3] + part[1], part[7], part[4], part[5]]
-    return sent, 2 * size, stages, part[0]
+    stages = [
+        (part[0] + part[6] + part[2], part[0]),
+        (part[3] + part[1], part[6] + part[2]),
+        (part[7], part[3] + part[1]),
+        (part[4], part[7]),
+        ([], part[4]),
+        (part[5], []),
+        ([], part[5]),
+    ]
+    return sent, size, stages
 
 
 def body(embeddings, cluster_ids, owner_map):
@@ -343,7 +367,7 @@
     capacity = items // pairs
     per_pair = clusters // pairs
     ids = cluster_ids.reshape(items // LANES, LANES)
-    sent, head, stages, local = plan(pairs)
+    sent, head, stages = plan(pairs)
     *blocks, pair, rank, label, table, slot, rows = first_blocks(
         ids, owner_map.reshape(1, clusters), embeddings, sent[:head], pairs, capacity
     )
@@ -355,29 +379,25 @@
         own[m] = blocks[m]
         if m:
             own[m] = lax.ppermute(own[m], "owner", [(d, d ^ (2 * m)) for d in range(owners)])
-    order = tuple(m for new in stages for m in new)
+    order = tuple(m for new, _ in stages for m in new)
     for m in order:
         other[m] = lax.ppermute(own[m], "owner", swap)
     state, mine, theirs = None, 0, 0
-    waiting = local
-    for new in stages + [[]]:
-        last = None if new else dict(numbers=order, per_pair=per_pair)
-        own_range, other_range = (mine, mine + len(new)), (theirs, theirs + len(waiting))
-        result = stage(
+    for index, (new, swapped) in enumerate(stages):
+        final = index == len(stages) - 1
+        state = stage(
             [own[m] for m in new],
-            [other[m] for m in waiting],
-            own_range,
-            other_range,
+            [other[m] for m in swapped],
+            (mine, mine + len(new)),
+            (theirs, theirs + len(swapped)),
             state,
             items,
             width,
             capacity,
-            last,
+            dict(numbers=order, per_pair=per_pair) if final else None,
         )
-        state = result[:3]
-        mine, theirs = own_range[1], other_range[1]
-        waiting = list(order[theirs:mine])
-    back = lax.all_to_all(result[3], "owner", split_axis=0, concat_axis=0, tiled=True)
+        mine, theirs = mine + len(new), theirs + len(swapped)
+    back = lax.all_to_all(state[-1], "owner", split_axis=0, concat_axis=0, tiled=True)
     maxima, mean = finish(back, pair, rank, table, clusters, pairs, per_pair)
     return maxima.reshape(items), mean.reshape(clusters)
 

time: 66.2 us -> 66.2 us (level)
    pallas_call x6 -> x7, Pallas kernels: 7.16 us -> 7.31 us  [stage(): pl.pallas_call(functools.partial(stage_kernel, own=own, other=other, fres...]
where the time goes in v2:
time: 66.2 us; the launch traced here: 66 us
  waiting for transfers between devices  21.9 us (33%)
  starting transfers between devices  21.4 us (32%)
  Pallas kernels  12.1 us (18%)
  blocking collectives  9.78 us (15%)
  between operations  0.75 us (1%)
    ppermute x7, waiting for transfers between devices, body(): lax.ppermute(own[m], 'owner', [(d, d ^ 2 * m) for d in range(owners)])  21.8 us
    ppermute x7, starting transfers between devices, body(): lax.ppermute(own[m], 'owner', [(d, d ^ 2 * m) for d in range(owners)])  20.3 us
    all_to_all x1, blocking collectives, body(): lax.all_to_all(state[-1], 'owner', split_axis=0, concat_axis=0, tiled=True)  9.78 us
    pallas_call x7, Pallas kernels, stage(): pl.pallas_call(functools.partial(stage_kernel, own=own, other=other, fres...  7.31 us
    pallas_call x1, Pallas kernels, later_blocks(): pl.pallas_call(functools.partial(later_kernel, numbers=numbers, capacity=...  2.21 us
    pallas_call x1, Pallas kernels, first_blocks(): pl.pallas_call(functools.partial(first_kernel, numbers=numbers, pairs=pai...  1.83 us
  transfers between devices with their start and end apart: 15, of which 4 were waited for; matrix products, arithmetic and copies ran while one was open for 0% of the time, Pallas kernels for 10%

profile of v2, /device:TPU:0, one launch (start us, length us, event | category | flops | bytes accessed | tf_op | source)
XLA Modules:
  0.0 66.0 jit_solution(18229781325659116703)
XLA Ops:
  0.6 1.8 %first.1 = (bf16[776,128]{1,0:T(8,128)(2,1)S(1)}, s32[8,128]{1,0:T(8,128)S(1)}, s32[8,128]{1,0:T(8,128)S(1)}, f32[8,128]{1,0:T(8,128)S(1)}, s32[8,128]{1,0:T(8,1...) custom-call(s32[8,128]{1,0:T(8,128)} %bitcast.10, s32[1,64]{1,0:T(1,128)} %bitcast.11, ...), custom_call_target="tpu_custom_call" | custom-call | tf_op jit(solution)/shard_map/first/pallas_call | solution.py:141
  2.5 2.2 %later.1 = (bf16[776,128]{1,0:T(8,128)(2,1)S(1)}, bf16[776,128]{1,0:T(8,128)(2,1)S(1)}, bf16[776,128]{1,0:T(8,128)(2,1)S(1)}, bf16[776,128]{1,0:T(8,128)(2,1)S(1...) custom-call(f32[64,128]{1,0:T(8,128)S(1)} %get-tuple-element.43.slot_ref, ...), custom_call_target="tpu_custom_call" | custom-call | tf_op jit(solution)/shard_map/later/pallas_call | solution.py:173
  4.7 3.1 %collective-permute-start.12 = (bf16[776,128]{1,0:T(8,128)(2,1)S(1)}, bf16[776,128]{1,0:T(8,128)(2,1)S(1)}, u32[]{:S(2)}, u32[]{:S(2)}) collective-permute-start(bf16[776,128]{1,0:T(8,128)(2,1)S(1)} %get-tuple-element.52), channel_id=1, source_target_pairs={{0,4},{1,5},{2,6},{3,7},{4,0},{5,1},{6,2},{7,3},{8,12},{9,13},{10,... | collective-permute-start | bytes 595976 | tf_op jit(solution)/shard_map/ppermute | solution.py:381
  7.8 0.0 collective-permute-start.14
  7.8 2.5 %collective-permute-start.10 = (bf16[776,128]{1,0:T(8,128)(2,1)S(1)}, bf16[776,128]{1,0:T(8,128)(2,1)S(1)}, u32[]{:S(2)}, u32[]{:S(2)}) collective-permute-start(bf16[776,128]{1,0:T(8,128)(2,1)S(1)} %get-tuple-element.51), channel_id=1, source_target_pairs={{0,12},{1,13},{2,14},{3,15},{4,8},{5,9},{6,10},{7,11},{8,4},{9,5},... | collective-permute-start | bytes 595976 | tf_op jit(solution)/shard_map/ppermute | solution.py:381
  10.3 1.6 %collective-permute-start.6 = (bf16[776,128]{1,0:T(8,128)(2,1)S(1)}, bf16[776,128]{1,0:T(8,128)(2,1)S(1)}, u32[]{:S(2)}, u32[]{:S(2)}) collective-permute-start(bf16[776,128]{1,0:T(8,128)(2,1)S(1)} %get-tuple-element.49), channel_id=1, source_target_pairs={{0,6},{1,7},{2,4},{3,5},{4,2},{5,3},{6,0},{7,1},{8,14},{9,15},{10,... | collective-permute-start | bytes 595976 | tf_op jit(solution)/shard_map/ppermute | solution.py:381
  11.9 0.5 collective-permute-start.8
  12.4 0.7 %collective-permute-done.12.refs_2_ = bf16[776,128]{1,0:T(8,128)(2,1)S(1)} collective-permute-done((bf16[776,128]{1,0:T(8,128)(2,1)S(1)}, bf16[776,128]{1,0:T(8,128)(2,1)S(1)}, u32[]{:S(2)}, u32[]{:S(2)}) %collective-permute-start.12) | collective-permute-done | bytes 198688 | tf_op jit(solution)/shard_map/ppermute | solution.py:381
  13.1 9.7 %collective-permute-start.4 = (bf16[776,128]{1,0:T(8,128)(2,1)S(1)}, bf16[776,128]{1,0:T(8,128)(2,1)S(1)}, u32[]{:S(2)}, u32[]{:S(2)}) collective-permute-start(bf16[776,128]{1,0:T(8,128)(2,1)S(1)} %get-tuple-element.48), channel_id=1, source_target_pairs={{0,14},{1,15},{2,12},{3,13},{4,10},{5,11},{6,8},{7,9},{8,6},{9,7},... | collective-permute-start | bytes 595976 | tf_op jit(solution)/shard_map/ppermute | solution.py:381
  22.9 0.0 collective-permute-start.2
  22.9 0.0 collective-permute-done.10.refs_1_
  22.9 2.9 %collective-permute-start = (bf16[776,128]{1,0:T(8,128)(2,1)S(1)}, bf16[776,128]{1,0:T(8,128)(2,1)S(1)}, u32[]{:S(2)}, u32[]{:S(2)}) collective-permute-start(bf16[776,128]{1,0:T(8,128)(2,1)S(1)} %get-tuple-element.46), channel_id=1, source_target_pairs={{0,10},{1,11},{2,8},{3,9},{4,14},{5,15},{6,12},{7,13},{8,2},{9,3},... | collective-permute-start | bytes 595976 | tf_op jit(solution)/shard_map/ppermute | solution.py:381
  25.7 0.0 collective-permute-done.6.refs_0_
  25.7 0.5 collective-permute-start.11
  26.3 3.7 %collective-permute-done.4.refs_0_ = bf16[776,128]{1,0:T(8,128)(2,1)S(1)} collective-permute-done((bf16[776,128]{1,0:T(8,128)(2,1)S(1)}, bf16[776,128]{1,0:T(8,128)(2,1)S(1)}, u32[]{:S(2)}, u32[]{:S(2)}) %collective-permute-start.4) | collective-permute-done | bytes 198688 | tf_op jit(solution)/shard_map/ppermute | solution.py:381
  30.0 0.0 collective-permute-start.7
  30.0 13.2 %collective-permute-done.2.refs_0_ = bf16[776,128]{1,0:T(8,128)(2,1)S(1)} collective-permute-done((bf16[776,128]{1,0:T(8,128)(2,1)S(1)}, bf16[776,128]{1,0:T(8,128)(2,1)S(1)}, u32[]{:S(2)}, u32[]{:S(2)}) %collective-permute-start.2) | collective-permute-done | bytes 198688 | tf_op jit(solution)/shard_map/ppermute | solution.py:381
  43.2 0.0 collective-permute-start.9
  43.2 4.2 %collective-permute-done.refs_0_ = bf16[776,128]{1,0:T(8,128)(2,1)S(1)} collective-permute-done((bf16[776,128]{1,0:T(8,128)(2,1)S(1)}, bf16[776,128]{1,0:T(8,128)(2,1)S(1)}, u32[]{:S(2)}, u32[]{:S(2)}) %collective-permute-start) | collective-permute-done | bytes 198688 | tf_op jit(solution)/shard_map/ppermute | solution.py:381
  47.4 0.0 collective-permute-start.5
  47.4 0.0 collective-permute-done.13.refs_3_
  47.4 0.5 collective-permute-start.3
  47.9 0.1 collective-permute-start.1
  48.0 0.7 %stage.7 = (bf16[2048,768]{1,0:T(8,128)(2,1)S(1)}, f32[8,2048]{1,0:T(8,128)S(1)}, f32[2048,128]{1,0:T(8,128)S(1)}, f32[8,1024]{1,0:T(8,128)S(1)}) custom-call(bf16[776,128]{1,0:T(8,128)(2,1)S(1)} %get-tuple-element.53.refs_0_, bf16[776,128]{1,0:T(8,128)(2,1)S(1)} %collective-permute-done.10.refs_1_, bf16[776,128]{1,0:T(8,128)(2,1)S(1)} %collective-permute-done.12.refs_2_, ...), custom_call_target="tpu_custom_call" | custom-call | tf_op jit(solution)/shard_map/stage/pallas_call | solution.py:288
  48.7 1.1 %stage.8 = (bf16[2048,768]{1,0:T(8,128)(2,1)S(1)}, f32[8,2048]{1,0:T(8,128)S(1)}, f32[2048,128]{1,0:T(8,128)S(1)}, f32[8,1024]{1,0:T(8,128)S(1)}) custom-call(bf16[776,128]{1,0:T(8,128)(2,1)S(1)} %collective-permute-done.6.refs_0_, ...), custom_call_target="tpu_custom_call", output_to_operand_aliasing={{0}: (4, {}), {1}: (5, {}), {2}: (6, {}), {3}: (7, {})} | custom-call | tf_op jit(solution)/shard_map/stage/pallas_call | solution.py:288
  49.9 1.3 %stage.9 = (bf16[2048,768]{1,0:T(8,128)(2,1)S(1)}, f32[8,2048]{1,0:T(8,128)S(1)}, f32[2048,128]{1,0:T(8,128)S(1)}, f32[8,1024]{1,0:T(8,128)S(1)}) custom-call(bf16[776,128]{1,0:T(8,128)(2,1)S(1)} %collective-permute-done.4.refs_0_, ...), custom_call_target="tpu_custom_call", output_to_operand_aliasing={{0}: (3, {}), {1}: (4, {}), {2}: (5, {}), {3}: (6, {})} | custom-call | tf_op jit(solution)/shard_map/stage/pallas_call | solution.py:288
  51.2 1.5 %stage.10 = (bf16[2048,768]{1,0:T(8,128)(2,1)S(1)}, f32[8,2048]{1,0:T(8,128)S(1)}, f32[2048,128]{1,0:T(8,128)S(1)}, f32[8,1024]{1,0:T(8,128)S(1)}) custom-call(bf16[776,128]{1,0:T(8,128)(2,1)S(1)} %collective-permute-done.2.refs_0_, ...), custom_call_target="tpu_custom_call", output_to_operand_aliasing={{0}: (2, {}), {1}: (3, {}), {2}: (4, {}), {3}: (5, {})} | custom-call | tf_op jit(solution)/shard_map/stage/pallas_call | solution.py:288
  52.7 0.6 stage.11
  53.3 1.3 %stage.12 = (bf16[2048,768]{1,0:T(8,128)(2,1)S(1)}, f32[8,2048]{1,0:T(8,128)S(1)}, f32[2048,128]{1,0:T(8,128)S(1)}, f32[8,1024]{1,0:T(8,128)S(1)}) custom-call(bf16[776,128]{1,0:T(8,128)(2,1)S(1)} %collective-permute-done.refs_0_, ...), custom_call_target="tpu_custom_call", output_to_operand_aliasing={{0}: (1, {}), {1}: (2, {}), {2}: (3, {}), {3}: (4, {})} | custom-call | tf_op jit(solution)/shard_map/stage/pallas_call | solution.py:288
  54.6 0.8 %stage.13 = (bf16[2048,768]{1,0:T(8,128)(2,1)S(1)}, f32[8,2048]{1,0:T(8,128)S(1)}, f32[2048,128]{1,0:T(8,128)S(1)}, f32[8,1024]{1,0:T(8,128)S(1)}, f32[16,256]{1,0:T(8,128)S(1)}) custom-call(bf16[776,128]{1,0:T(8,128)(2,1)S(1)} %collective-permute-done.1.refs_0_, ...), custom_call_target="tpu_custom_call", output_to_operand_aliasing={{0}: (1, {}), {1}: (2, {}), {2}: (3, {}), {3}: (4, {})} | custom-call | tf_op jit(solution)/shard_map/stage/pallas_call | solution.py:288
  55.4 9.8 %all_to_all.11 = f32[16,1,256]{2,1,0:T(1,128)S(1)} all-to-all(f32[16,1,256]{2,1,0:T(1,128)S(1)} %copy.29), channel_id=1, replica_groups=mesh['parts'=2,'owner'=16] {'owner'}, dimensions={0} | all-to-all | bytes 32768 | tf_op jit(solution)/shard_map/all_to_all | solution.py:400
  65.2 0.7 %finish.1 = (f32[8,128]{1,0:T(8,128)}, f32[1,64]{1,0:T(1,128)}) custom-call(f32[16,256]{1,0:T(8,128)S(1)} %bitcast.8, s32[8,128]{1,0:T(8,128)S(1)} %get-tuple-element.79.pair_ref, s32[8,128]{1,0:T(8,128)S(1)} %get-tuple-element.80.rank_ref, s32[8,128]{1,0:T(8,128)S(1)} %get-tuple-element.81.table_ref), custom_call_target="tpu_custom_call" | custom-call | tf_op jit(solution)/shard_map/finish/pallas_call | solution.py:333
  (11 shorter events, 0.0 us)
Async XLA Ops:
  4.7 8.4 %collective-permute-start.12 = (bf16[776,128]{1,0:T(8,128)(2,1)S(1)}, bf16[776,128]{1,0:T(8,128)(2,1)S(1)}, u32[]{:S(2)}, u32[]{:S(2)}) collective-permute-start(bf16[776,128]{1,0:T(8,128)(2,1)S(1)} %get-tuple-element.52), channel_id=1, source_target_pairs={{0,4},{1,5},{2,6},{3,7},{4,0},{5,1},{6,2},{7,3},{8,12},{9,13},{10,... | collective-permute-start | bytes 595976 | tf_op jit(solution)/shard_map/ppermute | solution.py:381
  7.8 15.1 %collective-permute-start.14 = (bf16[776,128]{1,0:T(8,128)(2,1)S(1)}, bf16[776,128]{1,0:T(8,128)(2,1)S(1)}, u32[]{:S(2)}, u32[]{:S(2)}) collective-permute-start(bf16[776,128]{1,0:T(8,128)(2,1)S(1)} %get-tuple-element.53.refs_0_), channel_id=1, source_target_pairs={{0,1},{1,0},{2,3},{3,2},{4,5},{5,4},{6,7},{7,6},{8,9},{9,8},{10,11... | collective-permute-start | bytes 595976 | tf_op jit(solution)/shard_map/ppermute | solution.py:384
  7.8 15.1 %collective-permute-start.10 = (bf16[776,128]{1,0:T(8,128)(2,1)S(1)}, bf16[776,128]{1,0:T(8,128)(2,1)S(1)}, u32[]{:S(2)}, u32[]{:S(2)}) collective-permute-start(bf16[776,128]{1,0:T(8,128)(2,1)S(1)} %get-tuple-element.51), channel_id=1, source_target_pairs={{0,12},{1,13},{2,14},{3,15},{4,8},{5,9},{6,10},{7,11},{8,4},{9,5},... | collective-permute-start | bytes 595976 | tf_op jit(solution)/shard_map/ppermute | solution.py:381
  10.3 15.5 %collective-permute-start.6 = (bf16[776,128]{1,0:T(8,128)(2,1)S(1)}, bf16[776,128]{1,0:T(8,128)(2,1)S(1)}, u32[]{:S(2)}, u32[]{:S(2)}) collective-permute-start(bf16[776,128]{1,0:T(8,128)(2,1)S(1)} %get-tuple-element.49), channel_id=1, source_target_pairs={{0,6},{1,7},{2,4},{3,5},{4,2},{5,3},{6,0},{7,1},{8,14},{9,15},{10,... | collective-permute-start | bytes 595976 | tf_op jit(solution)/shard_map/ppermute | solution.py:381
  11.9 13.8 %collective-permute-start.8 = (bf16[776,128]{1,0:T(8,128)(2,1)S(1)}, bf16[776,128]{1,0:T(8,128)(2,1)S(1)}, u32[]{:S(2)}, u32[]{:S(2)}) collective-permute-start(bf16[776,128]{1,0:T(8,128)(2,1)S(1)} %get-tuple-element.50), channel_id=1, source_target_pairs={{0,2},{1,3},{2,0},{3,1},{4,6},{5,7},{6,4},{7,5},{8,10},{9,11},{10,... | collective-permute-start | bytes 595976 | tf_op jit(solution)/shard_map/ppermute | solution.py:381
  13.1 16.9 %collective-permute-start.4 = (bf16[776,128]{1,0:T(8,128)(2,1)S(1)}, bf16[776,128]{1,0:T(8,128)(2,1)S(1)}, u32[]{:S(2)}, u32[]{:S(2)}) collective-permute-start(bf16[776,128]{1,0:T(8,128)(2,1)S(1)} %get-tuple-element.48), channel_id=1, source_target_pairs={{0,14},{1,15},{2,12},{3,13},{4,10},{5,11},{6,8},{7,9},{8,6},{9,7},... | collective-permute-start | bytes 595976 | tf_op jit(solution)/shard_map/ppermute | solution.py:381
  22.9 20.3 %collective-permute-start.2 = (bf16[776,128]{1,0:T(8,128)(2,1)S(1)}, bf16[776,128]{1,0:T(8,128)(2,1)S(1)}, u32[]{:S(2)}, u32[]{:S(2)}) collective-permute-start(bf16[776,128]{1,0:T(8,128)(2,1)S(1)} %get-tuple-element.47), channel_id=1, source_target_pairs={{0,8},{1,9},{2,10},{3,11},{4,12},{5,13},{6,14},{7,15},{8,0},{9,1},... | collective-permute-start | bytes 595976 | tf_op jit(solution)/shard_map/ppermute | solution.py:381
  22.9 24.5 %collective-permute-start = (bf16[776,128]{1,0:T(8,128)(2,1)S(1)}, bf16[776,128]{1,0:T(8,128)(2,1)S(1)}, u32[]{:S(2)}, u32[]{:S(2)}) collective-permute-start(bf16[776,128]{1,0:T(8,128)(2,1)S(1)} %get-tuple-element.46), channel_id=1, source_target_pairs={{0,10},{1,11},{2,8},{3,9},{4,14},{5,15},{6,12},{7,13},{8,2},{9,3},... | collective-permute-start | bytes 595976 | tf_op jit(solution)/shard_map/ppermute | solution.py:381
  25.7 21.7 %collective-permute-start.13 = (bf16[776,128]{1,0:T(8,128)(2,1)S(1)}, bf16[776,128]{1,0:T(8,128)(2,1)S(1)}, u32[]{:S(2)}, u32[]{:S(2)}) collective-permute-start(bf16[776,128]{1,0:T(8,128)(2,1)S(1)} %collective-permute-done.12.refs_2_), channel_id=1, source_target_pairs={{0,1},{1,0},{2,3},{3,2},{4,5},{5,4},{6,7},{7,6},{8,9},{9,8},{10,11... | collective-permute-start | bytes 595976 | tf_op jit(solution)/shard_map/ppermute | solution.py:384
  25.7 22.2 %collective-permute-start.11 = (bf16[776,128]{1,0:T(8,128)(2,1)S(1)}, bf16[776,128]{1,0:T(8,128)(2,1)S(1)}, u32[]{:S(2)}, u32[]{:S(2)}) collective-permute-start(bf16[776,128]{1,0:T(8,128)(2,1)S(1)} %collective-permute-done.10.refs_1_), channel_id=1, source_target_pairs={{0,1},{1,0},{2,3},{3,2},{4,5},{5,4},{6,7},{7,6},{8,9},{9,8},{10,11... | collective-permute-start | bytes 595976 | tf_op jit(solution)/shard_map/ppermute | solution.py:384
  30.0 19.8 %collective-permute-start.7 = (bf16[776,128]{1,0:T(8,128)(2,1)S(1)}, bf16[776,128]{1,0:T(8,128)(2,1)S(1)}, u32[]{:S(2)}, u32[]{:S(2)}) collective-permute-start(bf16[776,128]{1,0:T(8,128)(2,1)S(1)} %collective-permute-done.6.refs_0_), channel_id=1, source_target_pairs={{0,1},{1,0},{2,3},{3,2},{4,5},{5,4},{6,7},{7,6},{8,9},{9,8},{10,11... | collective-permute-start | bytes 595976 | tf_op jit(solution)/shard_map/ppermute | solution.py:384
  43.2 6.7 %collective-permute-start.9 = (bf16[776,128]{1,0:T(8,128)(2,1)S(1)}, bf16[776,128]{1,0:T(8,128)(2,1)S(1)}, u32[]{:S(2)}, u32[]{:S(2)}) collective-permute-start(bf16[776,128]{1,0:T(8,128)(2,1)S(1)} %collective-permute-done.8.refs_1_), channel_id=1, source_target_pairs={{0,1},{1,0},{2,3},{3,2},{4,5},{5,4},{6,7},{7,6},{8,9},{9,8},{10,11... | collective-permute-start | bytes 595976 | tf_op jit(solution)/shard_map/ppermute | solution.py:384
  47.4 3.8 %collective-permute-start.5 = (bf16[776,128]{1,0:T(8,128)(2,1)S(1)}, bf16[776,128]{1,0:T(8,128)(2,1)S(1)}, u32[]{:S(2)}, u32[]{:S(2)}) collective-permute-start(bf16[776,128]{1,0:T(8,128)(2,1)S(1)} %collective-permute-done.4.refs_0_), channel_id=1, source_target_pairs={{0,1},{1,0},{2,3},{3,2},{4,5},{5,4},{6,7},{7,6},{8,9},{9,8},{10,11... | collective-permute-start | bytes 595976 | tf_op jit(solution)/shard_map/ppermute | solution.py:384
  47.4 5.3 %collective-permute-start.3 = (bf16[776,128]{1,0:T(8,128)(2,1)S(1)}, bf16[776,128]{1,0:T(8,128)(2,1)S(1)}, u32[]{:S(2)}, u32[]{:S(2)}) collective-permute-start(bf16[776,128]{1,0:T(8,128)(2,1)S(1)} %collective-permute-done.2.refs_0_), channel_id=1, source_target_pairs={{0,1},{1,0},{2,3},{3,2},{4,5},{5,4},{6,7},{7,6},{8,9},{9,8},{10,11... | collective-permute-start | bytes 595976 | tf_op jit(solution)/shard_map/ppermute | solution.py:384
  47.9 6.7 %collective-permute-start.1 = (bf16[776,128]{1,0:T(8,128)(2,1)S(1)}, bf16[776,128]{1,0:T(8,128)(2,1)S(1)}, u32[]{:S(2)}, u32[]{:S(2)}) collective-permute-start(bf16[776,128]{1,0:T(8,128)(2,1)S(1)} %collective-permute-done.refs_0_), channel_id=1, source_target_pairs={{0,1},{1,0},{2,3},{3,2},{4,5},{5,4},{6,7},{7,6},{8,9},{9,8},{10,11... | collective-permute-start | bytes 595976 | tf_op jit(solution)/shard_map/ppermute | solution.py:384

commit v3 on v2

--- a/solution.py
+++ b/solution.py
@@ -195,7 +195,7 @@
     ].astype(F32)[0:1, :]
 
 
-def stage_kernel(*refs, own, other, fresh, items, capacity, last):
+def stage_kernel(*refs, own, other, fresh, items, capacity, per_pair, last):
     refs = list(refs)
     blocks = [refs.pop(0) for _ in range(own[1] - own[0] + other[1] - other[0])]
     if not fresh:
@@ -235,15 +235,60 @@
                     top = jnp.max(piece.reshape(LANES // 8, 8, LANES), axis=0)
                     best[t] = jnp.maximum(best[t], top)
 
-    meet(0, total, old, total)
-    meet(tiles, total_other, old, total)
-    meet(old, total, 0, old)
+    def face(tile, left, right):
+        across = jnp.full((LANES, LANES), -1.0, F32)
+        column = columns[span(tile, tile + 1), :]
+        for low in range(left, right, 8):
+            high = min(low + 8, right)
+            gram = lax.dot_general(
+                keys[span(tile, tile + 1), :],
+                keys[span(low, high), :],
+                (((1,), (1,)), ((), ())),
+                preferred_element_type=F32,
+            )
+            for t in range(low, high):
+                same = column == marks[0:1, span(t, t + 1)]
+                if t == tile:
+                    same = same & (iota((LANES, LANES), 0) != iota((LANES, LANES), 1))
+                piece = jnp.where(same, gram[:, span(t - low, t - low + 1)], -1.0)
+                across = jnp.maximum(across, piece)
+                if t < old:
+                    top = jnp.max(piece.reshape(LANES // 8, 8, LANES), axis=0)
+                    best[t] = jnp.maximum(best[t], top)
+        top = jnp.max(across.T.reshape(LANES // 8, 8, LANES), axis=0)
+        best[tile] = jnp.maximum(best[tile], top)
+
+    if total - old == 1:
+        face(old, 0, total)
+        face(old, tiles, total_other)
+    else:
+        meet(0, total, old, total)
+        meet(tiles, total_other, old, total)
+        meet(old, total, 0, old)
     meet(old_other, total_other, 0, old)
+    if total == tiles and old < tiles:
+        count(marks, tiles, per_pair)
     if last is None:
         for t in range(total):
             state[:, span(t, t + 1)] = best[t]
     else:
-        settle(best, marks, refs[4], capacity, **last)
+        settle(best, marks, refs[4], capacity, last, per_pair)
+
+
+def lay(values, first):
+    total = jnp.sum(values, axis=1, keepdims=True)
+    shape = (values.shape[0], LANES)
+    return jnp.sum(jnp.where(iota(shape, 0) + first == iota(shape, 1), total, 0.0), axis=0, keepdims=True)
+
+
+def labels_of(marks, tiles):
+    return jnp.concatenate([marks[0:1, span(t, t + 1)] for t in range(tiles)], axis=0)
+
+
+def count(marks, tiles, per_pair):
+    mark = labels_of(marks, tiles)
+    found = [jnp.sum((mark == k).astype(F32), axis=0, keepdims=True) for k in range(per_pair)]
+    marks[1:2, 0:LANES] = lay(jnp.concatenate(found, axis=0), per_pair)
 
 
 def settle(best, marks, out_ref, capacity, numbers, per_pair):
@@ -251,16 +296,9 @@
     owner = lax.axis_index("owner")
     chip, core = owner // 2, owner % 2
     rows = [jnp.max(best[t], axis=0, keepdims=True) for t in range(tiles)]
-    row = jnp.concatenate(rows, axis=0)
-    mark = jnp.concatenate([marks[0:1, span(t, t + 1)] for t in range(tiles)], axis=0)
-    sums, counts = [], []
-    for k in range(per_pair):
-        mine = mark == k
-        sums.append(jnp.sum(jnp.where(mine, row, 0.0), axis=0, keepdims=True))
-        counts.append(jnp.sum(mine.astype(F32), axis=0, keepdims=True))
-    stats = jnp.sum(jnp.concatenate(sums + counts, axis=0), axis=1, keepdims=True)
-    stats = jnp.where(iota((2 * per_pair, LANES), 0) == iota((2 * per_pair, LANES), 1), stats, 0.0)
-    stats = jnp.sum(stats, axis=0, keepdims=True)
+    row, mark = jnp.concatenate(rows, axis=0), labels_of(marks, tiles)
+    sums = [jnp.sum(jnp.where(mark == k, row, 0.0), axis=0, keepdims=True) for k in range(per_pair)]
+    stats = lay(jnp.concatenate(sums, axis=0), 0) + marks[1:2, 0:LANES]
     out_ref[:, span(1, 2)] = jnp.broadcast_to(stats, (2 * pairs, LANES))
     target = iota((2 * pairs, LANES), 0)
     back = jnp.zeros((2 * pairs, LANES), F32)
@@ -272,7 +310,7 @@
     out_ref[:, span(0, 1)] = back
 
 
-def stage(new_own, new_other, own, other, state, items, width, capacity, last):
+def stage(new_own, new_other, own, other, state, items, width, capacity, per_pair, last):
     args = [near(b) for b in new_own + new_other]
     fresh = state is None
     out = [
@@ -284,7 +322,7 @@
     aliases = {} if fresh else {len(args) + k: k for k in range(len(out))}
     args += [] if fresh else [near(a) for a in state]
     if last is not None:
-        out.append(pltpu.VMEM((2 * len(last["numbers"]), 2 * LANES), F32))
+        out.append(pltpu.VMEM((2 * len(last), 2 * LANES), F32))
     return pl.pallas_call(
         functools.partial(
             stage_kernel,
@@ -293,6 +331,7 @@
             fresh=fresh,
             items=items,
             capacity=capacity,
+            per_pair=per_pair,
             last=last,
         ),
         in_specs=[VMEM] * len(args),
@@ -346,17 +385,18 @@
 def plan(pairs):
     size = pairs // 8
     part = [list(range(k * size, (k + 1) * size)) for k in range(8)]
-    sent = part[6] + part[7] + part[4] + part[5] + part[2] + part[3] + part[1] + part[0]
+    sent = part[6] + part[4] + part[5] + part[2] + part[7] + part[3] + part[1] + part[0]
     stages = [
         (part[0] + part[6] + part[2], part[0]),
         (part[3] + part[1], part[6] + part[2]),
-        (part[7], part[3] + part[1]),
-        (part[4], part[7]),
-        ([], part[4]),
-        (part[5], []),
+        (part[4], part[3] + part[1]),
+        (part[5], part[4]),
         ([], part[5]),
+        (part[7], []),
+        ([], part[7]),
     ]
-    return sent, size, stages
+    groups = [sent[:size], sent[size:]]
+    return groups, stages
 
 
 def body(embeddings, cluster_ids, owner_map):
@@ -367,11 +407,13 @@
     capacity = items // pairs
     per_pair = clusters // pairs
     ids = cluster_ids.reshape(items // LANES, LANES)
-    sent, head, stages = plan(pairs)
+    groups, stages = plan(pairs)
+    sent = [m for made in groups for m in made]
     *blocks, pair, rank, label, table, slot, rows = first_blocks(
-        ids, owner_map.reshape(1, clusters), embeddings, sent[:head], pairs, capacity
+        ids, owner_map.reshape(1, clusters), embeddings, groups[0], pairs, capacity
     )
-    blocks += later_blocks(slot, label, rows, sent[head:], capacity)
+    for made in groups[1:]:
+        blocks += later_blocks(slot, label, rows, made, capacity)
     blocks = dict(zip(sent, blocks))
     swap = [(d, d ^ 1) for d in range(owners)]
     own, other = {}, {}
@@ -394,7 +436,8 @@
             items,
             width,
             capacity,
-            dict(numbers=order, per_pair=per_pair) if final else None,
+            per_pair,
+            order if final else None,
         )
         mine, theirs = mine + len(new), theirs + len(swapped)
     back = lax.all_to_all(state[-1], "owner", split_axis=0, concat_axis=0, tiled=True)

time: 66.2 us -> 64.6 us (0.976)
  waiting for transfers between devices: 21.9 us -> 17.9 us
  blocking collectives: 9.78 us -> 12.3 us
    ppermute x7, waiting for transfers between devices: 21.8 us -> 17.9 us  [body(): lax.ppermute(own[m], 'owner', [(d, d ^ 2 * m) for d in range(owners)])]
    all_to_all x1, blocking collectives: 9.78 us -> 12.3 us  [body(): lax.all_to_all(state[-1], 'owner', split_axis=0, concat_axis=0, tiled=True)]
  transfers between devices with their start and end apart: 15 -> 15, of which waited for: 4 -> 4; matrix products, arithmetic and copies ran while one was open for 0% -> 0% of each run, Pallas kernels for 10% -> 9%
where the time goes in v3:
time: 64.6 us; the launch traced here: 64.4 us
  starting transfers between devices  21.9 us (34%)
  waiting for transfers between devices  17.9 us (28%)
  blocking collectives  12.3 us (19%)
  Pallas kernels  11.5 us (18%)
  between operations  0.74 us (1%)
    ppermute x7, starting transfers between devices, body(): lax.ppermute(own[m], 'owner', [(d, d ^ 2 * m) for d in range(owners)])  20.4 us
    ppermute x7, waiting for transfers between devices, body(): lax.ppermute(own[m], 'owner', [(d, d ^ 2 * m) for d in range(owners)])  17.9 us
    all_to_all x1, blocking collectives, body(): lax.all_to_all(state[-1], 'owner', split_axis=0, concat_axis=0, tiled=True)  12.3 us
    pallas_call x7, Pallas kernels, stage(): pl.pallas_call(functools.partial(stage_kernel, own=own, other=other, fres...  6.7 us
    pallas_call x1, Pallas kernels, later_blocks(): pl.pallas_call(functools.partial(later_kernel, numbers=numbers, capacity=...  2.21 us
    pallas_call x1, Pallas kernels, first_blocks(): pl.pallas_call(functools.partial(first_kernel, numbers=numbers, pairs=pai...  1.83 us
    ppermute x8, starting transfers between devices, body(): other[m] = lax.ppermute(own[m], 'owner', swap)  1.54 us
  transfers between devices with their start and end apart: 15, of which 4 were waited for; matrix products, arithmetic and copies ran while one was open for 0% of the time, Pallas kernels for 9%

profile of v3, /device:TPU:0, one launch (start us, length us, event | category | flops | bytes accessed | tf_op | source)
XLA Modules:
  0.0 64.4 jit_solution(13990448256141459409)
XLA Ops:
  0.6 1.8 %first.1 = (bf16[776,128]{1,0:T(8,128)(2,1)S(1)}, s32[8,128]{1,0:T(8,128)S(1)}, s32[8,128]{1,0:T(8,128)S(1)}, f32[8,128]{1,0:T(8,128)S(1)}, s32[8,128]{1,0:T(8,1...) custom-call(s32[8,128]{1,0:T(8,128)} %bitcast.10, s32[1,64]{1,0:T(1,128)} %bitcast.11, ...), custom_call_target="tpu_custom_call" | custom-call | tf_op jit(solution)/shard_map/first/pallas_call | solution.py:141
  2.5 2.2 %later.1 = (bf16[776,128]{1,0:T(8,128)(2,1)S(1)}, bf16[776,128]{1,0:T(8,128)(2,1)S(1)}, bf16[776,128]{1,0:T(8,128)(2,1)S(1)}, bf16[776,128]{1,0:T(8,128)(2,1)S(1...) custom-call(f32[64,128]{1,0:T(8,128)S(1)} %get-tuple-element.43.slot_ref, ...), custom_call_target="tpu_custom_call" | custom-call | tf_op jit(solution)/shard_map/later/pallas_call | solution.py:173
  4.7 3.1 %collective-permute-start.12 = (bf16[776,128]{1,0:T(8,128)(2,1)S(1)}, bf16[776,128]{1,0:T(8,128)(2,1)S(1)}, u32[]{:S(2)}, u32[]{:S(2)}) collective-permute-start(bf16[776,128]{1,0:T(8,128)(2,1)S(1)} %get-tuple-element.52), channel_id=1, source_target_pairs={{0,4},{1,5},{2,6},{3,7},{4,0},{5,1},{6,2},{7,3},{8,12},{9,13},{10,... | collective-permute-start | bytes 595976 | tf_op jit(solution)/shard_map/ppermute | solution.py:423
  7.8 2.5 %collective-permute-start.10 = (bf16[776,128]{1,0:T(8,128)(2,1)S(1)}, bf16[776,128]{1,0:T(8,128)(2,1)S(1)}, u32[]{:S(2)}, u32[]{:S(2)}) collective-permute-start(bf16[776,128]{1,0:T(8,128)(2,1)S(1)} %get-tuple-element.51), channel_id=1, source_target_pairs={{0,12},{1,13},{2,14},{3,15},{4,8},{5,9},{6,10},{7,11},{8,4},{9,5},... | collective-permute-start | bytes 595976 | tf_op jit(solution)/shard_map/ppermute | solution.py:423
  10.3 1.6 %collective-permute-start.6 = (bf16[776,128]{1,0:T(8,128)(2,1)S(1)}, bf16[776,128]{1,0:T(8,128)(2,1)S(1)}, u32[]{:S(2)}, u32[]{:S(2)}) collective-permute-start(bf16[776,128]{1,0:T(8,128)(2,1)S(1)} %get-tuple-element.49), channel_id=1, source_target_pairs={{0,6},{1,7},{2,4},{3,5},{4,2},{5,3},{6,0},{7,1},{8,14},{9,15},{10,... | collective-permute-start | bytes 595976 | tf_op jit(solution)/shard_map/ppermute | solution.py:423
  11.9 0.5 collective-permute-start.8
  12.4 0.7 %collective-permute-done.12.refs_2_ = bf16[776,128]{1,0:T(8,128)(2,1)S(1)} collective-permute-done((bf16[776,128]{1,0:T(8,128)(2,1)S(1)}, bf16[776,128]{1,0:T(8,128)(2,1)S(1)}, u32[]{:S(2)}, u32[]{:S(2)}) %collective-permute-start.12) | collective-permute-done | bytes 198688 | tf_op jit(solution)/shard_map/ppermute | solution.py:423
  13.1 6.6 %collective-permute-start.4 = (bf16[776,128]{1,0:T(8,128)(2,1)S(1)}, bf16[776,128]{1,0:T(8,128)(2,1)S(1)}, u32[]{:S(2)}, u32[]{:S(2)}) collective-permute-start(bf16[776,128]{1,0:T(8,128)(2,1)S(1)} %get-tuple-element.48), channel_id=1, source_target_pairs={{0,8},{1,9},{2,10},{3,11},{4,12},{5,13},{6,14},{7,15},{8,0},{9,1},... | collective-permute-start | bytes 595976 | tf_op jit(solution)/shard_map/ppermute | solution.py:423
  19.7 1.0 %collective-permute-start.2 = (bf16[776,128]{1,0:T(8,128)(2,1)S(1)}, bf16[776,128]{1,0:T(8,128)(2,1)S(1)}, u32[]{:S(2)}, u32[]{:S(2)}) collective-permute-start(bf16[776,128]{1,0:T(8,128)(2,1)S(1)} %get-tuple-element.47), channel_id=1, source_target_pairs={{0,10},{1,11},{2,8},{3,9},{4,14},{5,15},{6,12},{7,13},{8,2},{9,3},... | collective-permute-start | bytes 595976 | tf_op jit(solution)/shard_map/ppermute | solution.py:423
  20.7 0.0 collective-permute-done.10.refs_1_
  20.7 5.1 %collective-permute-start = (bf16[776,128]{1,0:T(8,128)(2,1)S(1)}, bf16[776,128]{1,0:T(8,128)(2,1)S(1)}, u32[]{:S(2)}, u32[]{:S(2)}) collective-permute-start(bf16[776,128]{1,0:T(8,128)(2,1)S(1)} %get-tuple-element.46), channel_id=1, source_target_pairs={{0,14},{1,15},{2,12},{3,13},{4,10},{5,11},{6,8},{7,9},{8,6},{9,7},... | collective-permute-start | bytes 595976 | tf_op jit(solution)/shard_map/ppermute | solution.py:423
  25.7 0.1 collective-permute-done.6.refs_0_
  25.8 0.0 collective-permute-start.13
  25.9 0.5 collective-permute-start.11
  26.4 11.9 %collective-permute-done.4.refs_0_ = bf16[776,128]{1,0:T(8,128)(2,1)S(1)} collective-permute-done((bf16[776,128]{1,0:T(8,128)(2,1)S(1)}, bf16[776,128]{1,0:T(8,128)(2,1)S(1)}, u32[]{:S(2)}, u32[]{:S(2)}) %collective-permute-start.4) | collective-permute-done | bytes 198688 | tf_op jit(solution)/shard_map/ppermute | solution.py:423
  38.3 0.0 collective-permute-start.7
  38.3 5.2 %collective-permute-done.2.refs_0_ = bf16[776,128]{1,0:T(8,128)(2,1)S(1)} collective-permute-done((bf16[776,128]{1,0:T(8,128)(2,1)S(1)}, bf16[776,128]{1,0:T(8,128)(2,1)S(1)}, u32[]{:S(2)}, u32[]{:S(2)}) %collective-permute-start.2) | collective-permute-done | bytes 198688 | tf_op jit(solution)/shard_map/ppermute | solution.py:423
  43.5 0.0 collective-permute-start.9
  43.5 0.0 collective-permute-done.refs_0_
  43.5 0.5 collective-permute-start.5
  44.0 0.1 collective-permute-start.3
  44.1 0.0 collective-permute-done.11.refs_2_
  44.1 0.4 collective-permute-start.1
  44.5 0.7 %stage.7 = (bf16[2048,768]{1,0:T(8,128)(2,1)S(1)}, f32[8,2048]{1,0:T(8,128)S(1)}, f32[2048,128]{1,0:T(8,128)S(1)}, f32[8,1024]{1,0:T(8,128)S(1)}) custom-call(bf16[776,128]{1,0:T(8,128)(2,1)S(1)} %get-tuple-element.53.refs_0_, bf16[776,128]{1,0:T(8,128)(2,1)S(1)} %collective-permute-done.10.refs_1_, bf16[776,128]{1,0:T(8,128)(2,1)S(1)} %collective-permute-done.12.refs_2_, ...), custom_call_target="tpu_custom_call" | custom-call | tf_op jit(solution)/shard_map/stage/pallas_call | solution.py:326
  45.2 1.1 %stage.8 = (bf16[2048,768]{1,0:T(8,128)(2,1)S(1)}, f32[8,2048]{1,0:T(8,128)S(1)}, f32[2048,128]{1,0:T(8,128)S(1)}, f32[8,1024]{1,0:T(8,128)S(1)}) custom-call(bf16[776,128]{1,0:T(8,128)(2,1)S(1)} %collective-permute-done.6.refs_0_, ...), custom_call_target="tpu_custom_call", output_to_operand_aliasing={{0}: (4, {}), {1}: (5, {}), {2}: (6, {}), {3}: (7, {})} | custom-call | tf_op jit(solution)/shard_map/stage/pallas_call | solution.py:326
  46.3 1.2 %stage.9 = (bf16[2048,768]{1,0:T(8,128)(2,1)S(1)}, f32[8,2048]{1,0:T(8,128)S(1)}, f32[2048,128]{1,0:T(8,128)S(1)}, f32[8,1024]{1,0:T(8,128)S(1)}) custom-call(bf16[776,128]{1,0:T(8,128)(2,1)S(1)} %collective-permute-done.4.refs_0_, ...), custom_call_target="tpu_custom_call", output_to_operand_aliasing={{0}: (3, {}), {1}: (4, {}), {2}: (5, {}), {3}: (6, {})} | custom-call | tf_op jit(solution)/shard_map/stage/pallas_call | solution.py:326
  47.5 1.2 %stage.10 = (bf16[2048,768]{1,0:T(8,128)(2,1)S(1)}, f32[8,2048]{1,0:T(8,128)S(1)}, f32[2048,128]{1,0:T(8,128)S(1)}, f32[8,1024]{1,0:T(8,128)S(1)}) custom-call(bf16[776,128]{1,0:T(8,128)(2,1)S(1)} %collective-permute-done.2.refs_0_, ...), custom_call_target="tpu_custom_call", output_to_operand_aliasing={{0}: (2, {}), {1}: (3, {}), {2}: (4, {}), {3}: (5, {})} | custom-call | tf_op jit(solution)/shard_map/stage/pallas_call | solution.py:326
  48.8 0.6 stage.11
  49.4 1.2 %stage.12 = (bf16[2048,768]{1,0:T(8,128)(2,1)S(1)}, f32[8,2048]{1,0:T(8,128)S(1)}, f32[2048,128]{1,0:T(8,128)S(1)}, f32[8,1024]{1,0:T(8,128)S(1)}) custom-call(bf16[776,128]{1,0:T(8,128)(2,1)S(1)} %collective-permute-done.refs_0_, ...), custom_call_target="tpu_custom_call", output_to_operand_aliasing={{0}: (1, {}), {1}: (2, {}), {2}: (3, {}), {3}: (4, {})} | custom-call | tf_op jit(solution)/shard_map/stage/pallas_call | solution.py:326
  50.5 0.8 %stage.13 = (bf16[2048,768]{1,0:T(8,128)(2,1)S(1)}, f32[8,2048]{1,0:T(8,128)S(1)}, f32[2048,128]{1,0:T(8,128)S(1)}, f32[8,1024]{1,0:T(8,128)S(1)}, f32[16,256]{1,0:T(8,128)S(1)}) custom-call(bf16[776,128]{1,0:T(8,128)(2,1)S(1)} %collective-permute-done.1.refs_0_, ...), custom_call_target="tpu_custom_call", output_to_operand_aliasing={{0}: (1, {}), {1}: (2, {}), {2}: (3, {}), {3}: (4, {})} | custom-call | tf_op jit(solution)/shard_map/stage/pallas_call | solution.py:326
  51.3 12.3 %all_to_all.11 = f32[16,1,256]{2,1,0:T(1,128)S(1)} all-to-all(f32[16,1,256]{2,1,0:T(1,128)S(1)} %copy.29), channel_id=1, replica_groups=mesh['parts'=2,'owner'=16] {'owner'}, dimensions={0} | all-to-all | bytes 32768 | tf_op jit(solution)/shard_map/all_to_all | solution.py:443
  63.6 0.7 %finish.1 = (f32[8,128]{1,0:T(8,128)}, f32[1,64]{1,0:T(1,128)}) custom-call(f32[16,256]{1,0:T(8,128)S(1)} %bitcast.8, s32[8,128]{1,0:T(8,128)S(1)} %get-tuple-element.79.pair_ref, s32[8,128]{1,0:T(8,128)S(1)} %get-tuple-element.80.rank_ref, s32[8,128]{1,0:T(8,128)S(1)} %get-tuple-element.81.table_ref), custom_call_target="tpu_custom_call" | custom-call | tf_op jit(solution)/shard_map/finish/pallas_call | solution.py:372
  (11 shorter events, 0.0 us)
Async XLA Ops:
  4.7 8.4 %collective-permute-start.12 = (bf16[776,128]{1,0:T(8,128)(2,1)S(1)}, bf16[776,128]{1,0:T(8,128)(2,1)S(1)}, u32[]{:S(2)}, u32[]{:S(2)}) collective-permute-start(bf16[776,128]{1,0:T(8,128)(2,1)S(1)} %get-tuple-element.52), channel_id=1, source_target_pairs={{0,4},{1,5},{2,6},{3,7},{4,0},{5,1},{6,2},{7,3},{8,12},{9,13},{10,... | collective-permute-start | bytes 595976 | tf_op jit(solution)/shard_map/ppermute | solution.py:423
  7.8 11.9 %collective-permute-start.14 = (bf16[776,128]{1,0:T(8,128)(2,1)S(1)}, bf16[776,128]{1,0:T(8,128)(2,1)S(1)}, u32[]{:S(2)}, u32[]{:S(2)}) collective-permute-start(bf16[776,128]{1,0:T(8,128)(2,1)S(1)} %get-tuple-element.53.refs_0_), channel_id=1, source_target_pairs={{0,1},{1,0},{2,3},{3,2},{4,5},{5,4},{6,7},{7,6},{8,9},{9,8},{10,11... | collective-permute-start | bytes 595976 | tf_op jit(solution)/shard_map/ppermute | solution.py:426
  7.8 12.9 %collective-permute-start.10 = (bf16[776,128]{1,0:T(8,128)(2,1)S(1)}, bf16[776,128]{1,0:T(8,128)(2,1)S(1)}, u32[]{:S(2)}, u32[]{:S(2)}) collective-permute-start(bf16[776,128]{1,0:T(8,128)(2,1)S(1)} %get-tuple-element.51), channel_id=1, source_target_pairs={{0,12},{1,13},{2,14},{3,15},{4,8},{5,9},{6,10},{7,11},{8,4},{9,5},... | collective-permute-start | bytes 595976 | tf_op jit(solution)/shard_map/ppermute | solution.py:423
  10.3 15.6 %collective-permute-start.6 = (bf16[776,128]{1,0:T(8,128)(2,1)S(1)}, bf16[776,128]{1,0:T(8,128)(2,1)S(1)}, u32[]{:S(2)}, u32[]{:S(2)}) collective-permute-start(bf16[776,128]{1,0:T(8,128)(2,1)S(1)} %get-tuple-element.49), channel_id=1, source_target_pairs={{0,6},{1,7},{2,4},{3,5},{4,2},{5,3},{6,0},{7,1},{8,14},{9,15},{10,... | collective-permute-start | bytes 595976 | tf_op jit(solution)/shard_map/ppermute | solution.py:423
  11.9 13.9 %collective-permute-start.8 = (bf16[776,128]{1,0:T(8,128)(2,1)S(1)}, bf16[776,128]{1,0:T(8,128)(2,1)S(1)}, u32[]{:S(2)}, u32[]{:S(2)}) collective-permute-start(bf16[776,128]{1,0:T(8,128)(2,1)S(1)} %get-tuple-element.50), channel_id=1, source_target_pairs={{0,2},{1,3},{2,0},{3,1},{4,6},{5,7},{6,4},{7,5},{8,10},{9,11},{10,... | collective-permute-start | bytes 595976 | tf_op jit(solution)/shard_map/ppermute | solution.py:423
  13.1 25.2 %collective-permute-start.4 = (bf16[776,128]{1,0:T(8,128)(2,1)S(1)}, bf16[776,128]{1,0:T(8,128)(2,1)S(1)}, u32[]{:S(2)}, u32[]{:S(2)}) collective-permute-start(bf16[776,128]{1,0:T(8,128)(2,1)S(1)} %get-tuple-element.48), channel_id=1, source_target_pairs={{0,8},{1,9},{2,10},{3,11},{4,12},{5,13},{6,14},{7,15},{8,0},{9,1},... | collective-permute-start | bytes 595976 | tf_op jit(solution)/shard_map/ppermute | solution.py:423
  19.7 23.8 %collective-permute-start.2 = (bf16[776,128]{1,0:T(8,128)(2,1)S(1)}, bf16[776,128]{1,0:T(8,128)(2,1)S(1)}, u32[]{:S(2)}, u32[]{:S(2)}) collective-permute-start(bf16[776,128]{1,0:T(8,128)(2,1)S(1)} %get-tuple-element.47), channel_id=1, source_target_pairs={{0,10},{1,11},{2,8},{3,9},{4,14},{5,15},{6,12},{7,13},{8,2},{9,3},... | collective-permute-start | bytes 595976 | tf_op jit(solution)/shard_map/ppermute | solution.py:423
  20.7 22.8 %collective-permute-start = (bf16[776,128]{1,0:T(8,128)(2,1)S(1)}, bf16[776,128]{1,0:T(8,128)(2,1)S(1)}, u32[]{:S(2)}, u32[]{:S(2)}) collective-permute-start(bf16[776,128]{1,0:T(8,128)(2,1)S(1)} %get-tuple-element.46), channel_id=1, source_target_pairs={{0,14},{1,15},{2,12},{3,13},{4,10},{5,11},{6,8},{7,9},{8,6},{9,7},... | collective-permute-start | bytes 595976 | tf_op jit(solution)/shard_map/ppermute | solution.py:423
  25.8 18.1 %collective-permute-start.13 = (bf16[776,128]{1,0:T(8,128)(2,1)S(1)}, bf16[776,128]{1,0:T(8,128)(2,1)S(1)}, u32[]{:S(2)}, u32[]{:S(2)}) collective-permute-start(bf16[776,128]{1,0:T(8,128)(2,1)S(1)} %collective-permute-done.12.refs_2_), channel_id=1, source_target_pairs={{0,1},{1,0},{2,3},{3,2},{4,5},{5,4},{6,7},{7,6},{8,9},{9,8},{10,11... | collective-permute-start | bytes 595976 | tf_op jit(solution)/shard_map/ppermute | solution.py:426
  25.9 18.2 %collective-permute-start.11 = (bf16[776,128]{1,0:T(8,128)(2,1)S(1)}, bf16[776,128]{1,0:T(8,128)(2,1)S(1)}, u32[]{:S(2)}, u32[]{:S(2)}) collective-permute-start(bf16[776,128]{1,0:T(8,128)(2,1)S(1)} %collective-permute-done.10.refs_1_), channel_id=1, source_target_pairs={{0,1},{1,0},{2,3},{3,2},{4,5},{5,4},{6,7},{7,6},{8,9},{9,8},{10,11... | collective-permute-start | bytes 595976 | tf_op jit(solution)/shard_map/ppermute | solution.py:426
  38.3 8.1 %collective-permute-start.7 = (bf16[776,128]{1,0:T(8,128)(2,1)S(1)}, bf16[776,128]{1,0:T(8,128)(2,1)S(1)}, u32[]{:S(2)}, u32[]{:S(2)}) collective-permute-start(bf16[776,128]{1,0:T(8,128)(2,1)S(1)} %collective-permute-done.6.refs_0_), channel_id=1, source_target_pairs={{0,1},{1,0},{2,3},{3,2},{4,5},{5,4},{6,7},{7,6},{8,9},{9,8},{10,11... | collective-permute-start | bytes 595976 | tf_op jit(solution)/shard_map/ppermute | solution.py:426
  43.5 2.9 %collective-permute-start.9 = (bf16[776,128]{1,0:T(8,128)(2,1)S(1)}, bf16[776,128]{1,0:T(8,128)(2,1)S(1)}, u32[]{:S(2)}, u32[]{:S(2)}) collective-permute-start(bf16[776,128]{1,0:T(8,128)(2,1)S(1)} %collective-permute-done.8.refs_1_), channel_id=1, source_target_pairs={{0,1},{1,0},{2,3},{3,2},{4,5},{5,4},{6,7},{7,6},{8,9},{9,8},{10,11... | collective-permute-start | bytes 595976 | tf_op jit(solution)/shard_map/ppermute | solution.py:426
  43.5 4.0 %collective-permute-start.5 = (bf16[776,128]{1,0:T(8,128)(2,1)S(1)}, bf16[776,128]{1,0:T(8,128)(2,1)S(1)}, u32[]{:S(2)}, u32[]{:S(2)}) collective-permute-start(bf16[776,128]{1,0:T(8,128)(2,1)S(1)} %collective-permute-done.4.refs_0_), channel_id=1, source_target_pairs={{0,1},{1,0},{2,3},{3,2},{4,5},{5,4},{6,7},{7,6},{8,9},{9,8},{10,11... | collective-permute-start | bytes 595976 | tf_op jit(solution)/shard_map/ppermute | solution.py:426
  44.0 4.8 %collective-permute-start.3 = (bf16[776,128]{1,0:T(8,128)(2,1)S(1)}, bf16[776,128]{1,0:T(8,128)(2,1)S(1)}, u32[]{:S(2)}, u32[]{:S(2)}) collective-permute-start(bf16[776,128]{1,0:T(8,128)(2,1)S(1)} %collective-permute-done.2.refs_0_), channel_id=1, source_target_pairs={{0,1},{1,0},{2,3},{3,2},{4,5},{5,4},{6,7},{7,6},{8,9},{9,8},{10,11... | collective-permute-start | bytes 595976 | tf_op jit(solution)/shard_map/ppermute | solution.py:426
  44.1 6.5 %collective-permute-start.1 = (bf16[776,128]{1,0:T(8,128)(2,1)S(1)}, bf16[776,128]{1,0:T(8,128)(2,1)S(1)}, u32[]{:S(2)}, u32[]{:S(2)}) collective-permute-start(bf16[776,128]{1,0:T(8,128)(2,1)S(1)} %collective-permute-done.refs_0_), channel_id=1, source_target_pairs={{0,1},{1,0},{2,3},{3,2},{4,5},{5,4},{6,7},{7,6},{8,9},{9,8},{10,11... | collective-permute-start | bytes 595976 | tf_op jit(solution)/shard_map/ppermute | solution.py:426

commit v4 on v3

--- a/solution.py
+++ b/solution.py
@@ -385,15 +385,14 @@
 def plan(pairs):
     size = pairs // 8
     part = [list(range(k * size, (k + 1) * size)) for k in range(8)]
-    sent = part[6] + part[4] + part[5] + part[2] + part[7] + part[3] + part[1] + part[0]
+    sent = part[6] + part[4] + part[5] + part[2] + part[7] + part[1] + part[3] + part[0]
     stages = [
         (part[0] + part[6] + part[2], part[0]),
         (part[3] + part[1], part[6] + part[2]),
         (part[4], part[3] + part[1]),
         (part[5], part[4]),
-        ([], part[5]),
         (part[7], []),
-        ([], part[7]),
+        ([], part[5] + part[7]),
     ]
     groups = [sent[:size], sent[size:]]
     return groups, stages

time: 64.6 us -> 64 us (level)
  Pallas kernels: 11.5 us -> 10.8 us
    pallas_call x7 -> x6, Pallas kernels: 6.7 us -> 6.08 us  [stage(): pl.pallas_call(functools.partial(stage_kernel, own=own, other=other, fres...]
  transfers between devices with their start and end apart: 15 -> 15, of which waited for: 4 -> 4; matrix products, arithmetic and copies ran while one was open for 0% -> 0% of each run, Pallas kernels for 9% -> 8%
where the time goes in v4:
time: 64 us; the launch traced here: 63.8 us
  starting transfers between devices  21.9 us (34%)
  waiting for transfers between devices  17.9 us (28%)
  blocking collectives  12.3 us (19%)
  Pallas kernels  10.8 us (17%)
  between operations  0.74 us (1%)
    ppermute x7, starting transfers between devices, body(): lax.ppermute(own[m], 'owner', [(d, d ^ 2 * m) for d in range(owners)])  20.4 us
    ppermute x7, waiting for transfers between devices, body(): lax.ppermute(own[m], 'owner', [(d, d ^ 2 * m) for d in range(owners)])  17.9 us
    all_to_all x1, blocking collectives, body(): lax.all_to_all(state[-1], 'owner', split_axis=0, concat_axis=0, tiled=True)  12.3 us
    pallas_call x6, Pallas kernels, stage(): pl.pallas_call(functools.partial(stage_kernel, own=own, other=other, fres...  6.08 us
    pallas_call x1, Pallas kernels, later_blocks(): pl.pallas_call(functools.partial(later_kernel, numbers=numbers, capacity=...  2.21 us
    pallas_call x1, Pallas kernels, first_blocks(): pl.pallas_call(functools.partial(first_kernel, numbers=numbers, pairs=pai...  1.83 us
    ppermute x8, starting transfers between devices, body(): other[m] = lax.ppermute(own[m], 'owner', swap)  1.54 us
  transfers between devices with their start and end apart: 15, of which 4 were waited for; matrix products, arithmetic and copies ran while one was open for 0% of the time, Pallas kernels for 8%

profile of v4, /device:TPU:0, one launch (start us, length us, event | category | flops | bytes accessed | tf_op | source)
XLA Modules:
  0.0 63.8 jit_solution(6309524575685352298)
XLA Ops:
  0.6 1.8 %first.1 = (bf16[776,128]{1,0:T(8,128)(2,1)S(1)}, s32[8,128]{1,0:T(8,128)S(1)}, s32[8,128]{1,0:T(8,128)S(1)}, f32[8,128]{1,0:T(8,128)S(1)}, s32[8,128]{1,0:T(8,1...) custom-call(s32[8,128]{1,0:T(8,128)} %bitcast.10, s32[1,64]{1,0:T(1,128)} %bitcast.11, ...), custom_call_target="tpu_custom_call" | custom-call | tf_op jit(solution)/shard_map/first/pallas_call | solution.py:141
  2.5 2.2 %later.1 = (bf16[776,128]{1,0:T(8,128)(2,1)S(1)}, bf16[776,128]{1,0:T(8,128)(2,1)S(1)}, bf16[776,128]{1,0:T(8,128)(2,1)S(1)}, bf16[776,128]{1,0:T(8,128)(2,1)S(1...) custom-call(f32[64,128]{1,0:T(8,128)S(1)} %get-tuple-element.39.slot_ref, ...), custom_call_target="tpu_custom_call" | custom-call | tf_op jit(solution)/shard_map/later/pallas_call | solution.py:173
  4.7 3.1 %collective-permute-start.12 = (bf16[776,128]{1,0:T(8,128)(2,1)S(1)}, bf16[776,128]{1,0:T(8,128)(2,1)S(1)}, u32[]{:S(2)}, u32[]{:S(2)}) collective-permute-start(bf16[776,128]{1,0:T(8,128)(2,1)S(1)} %get-tuple-element.48), channel_id=1, source_target_pairs={{0,4},{1,5},{2,6},{3,7},{4,0},{5,1},{6,2},{7,3},{8,12},{9,13},{10,... | collective-permute-start | bytes 595976 | tf_op jit(solution)/shard_map/ppermute | solution.py:422
  7.8 0.0 collective-permute-start.14
  7.8 2.5 %collective-permute-start.10 = (bf16[776,128]{1,0:T(8,128)(2,1)S(1)}, bf16[776,128]{1,0:T(8,128)(2,1)S(1)}, u32[]{:S(2)}, u32[]{:S(2)}) collective-permute-start(bf16[776,128]{1,0:T(8,128)(2,1)S(1)} %get-tuple-element.47), channel_id=1, source_target_pairs={{0,12},{1,13},{2,14},{3,15},{4,8},{5,9},{6,10},{7,11},{8,4},{9,5},... | collective-permute-start | bytes 595976 | tf_op jit(solution)/shard_map/ppermute | solution.py:422
  10.3 1.6 %collective-permute-start.6 = (bf16[776,128]{1,0:T(8,128)(2,1)S(1)}, bf16[776,128]{1,0:T(8,128)(2,1)S(1)}, u32[]{:S(2)}, u32[]{:S(2)}) collective-permute-start(bf16[776,128]{1,0:T(8,128)(2,1)S(1)} %get-tuple-element.45), channel_id=1, source_target_pairs={{0,6},{1,7},{2,4},{3,5},{4,2},{5,3},{6,0},{7,1},{8,14},{9,15},{10,... | collective-permute-start | bytes 595976 | tf_op jit(solution)/shard_map/ppermute | solution.py:422
  11.9 0.5 collective-permute-start.8
  12.4 0.7 %collective-permute-done.12.refs_2_ = bf16[776,128]{1,0:T(8,128)(2,1)S(1)} collective-permute-done((bf16[776,128]{1,0:T(8,128)(2,1)S(1)}, bf16[776,128]{1,0:T(8,128)(2,1)S(1)}, u32[]{:S(2)}, u32[]{:S(2)}) %collective-permute-start.12) | collective-permute-done | bytes 198688 | tf_op jit(solution)/shard_map/ppermute | solution.py:422
  13.1 6.6 %collective-permute-start.4 = (bf16[776,128]{1,0:T(8,128)(2,1)S(1)}, bf16[776,128]{1,0:T(8,128)(2,1)S(1)}, u32[]{:S(2)}, u32[]{:S(2)}) collective-permute-start(bf16[776,128]{1,0:T(8,128)(2,1)S(1)} %get-tuple-element.44), channel_id=1, source_target_pairs={{0,8},{1,9},{2,10},{3,11},{4,12},{5,13},{6,14},{7,15},{8,0},{9,1},... | collective-permute-start | bytes 595976 | tf_op jit(solution)/shard_map/ppermute | solution.py:422
  19.7 0.0 collective-permute-done.14.refs_3_
  19.7 1.0 %collective-permute-start = (bf16[776,128]{1,0:T(8,128)(2,1)S(1)}, bf16[776,128]{1,0:T(8,128)(2,1)S(1)}, u32[]{:S(2)}, u32[]{:S(2)}) collective-permute-start(bf16[776,128]{1,0:T(8,128)(2,1)S(1)} %get-tuple-element.42), channel_id=1, source_target_pairs={{0,10},{1,11},{2,8},{3,9},{4,14},{5,15},{6,12},{7,13},{8,2},{9,3},... | collective-permute-start | bytes 595976 | tf_op jit(solution)/shard_map/ppermute | solution.py:422
  20.7 5.1 %collective-permute-start.2 = (bf16[776,128]{1,0:T(8,128)(2,1)S(1)}, bf16[776,128]{1,0:T(8,128)(2,1)S(1)}, u32[]{:S(2)}, u32[]{:S(2)}) collective-permute-start(bf16[776,128]{1,0:T(8,128)(2,1)S(1)} %get-tuple-element.43), channel_id=1, source_target_pairs={{0,14},{1,15},{2,12},{3,13},{4,10},{5,11},{6,8},{7,9},{8,6},{9,7},... | collective-permute-start | bytes 595976 | tf_op jit(solution)/shard_map/ppermute | solution.py:422
  25.7 0.1 collective-permute-done.6.refs_0_
  25.8 0.0 collective-permute-start.13
  25.8 0.0 collective-permute-done.8.refs_1_
  25.9 0.5 collective-permute-start.11
  26.4 11.9 %collective-permute-done.4.refs_0_ = bf16[776,128]{1,0:T(8,128)(2,1)S(1)} collective-permute-done((bf16[776,128]{1,0:T(8,128)(2,1)S(1)}, bf16[776,128]{1,0:T(8,128)(2,1)S(1)}, u32[]{:S(2)}, u32[]{:S(2)}) %collective-permute-start.4) | collective-permute-done | bytes 198688 | tf_op jit(solution)/shard_map/ppermute | solution.py:422
  38.3 5.2 %collective-permute-done.refs_0_ = bf16[776,128]{1,0:T(8,128)(2,1)S(1)} collective-permute-done((bf16[776,128]{1,0:T(8,128)(2,1)S(1)}, bf16[776,128]{1,0:T(8,128)(2,1)S(1)}, u32[]{:S(2)}, u32[]{:S(2)}) %collective-permute-start) | collective-permute-done | bytes 198688 | tf_op jit(solution)/shard_map/ppermute | solution.py:422
  43.5 0.0 collective-permute-start.9
  43.5 0.0 collective-permute-done.2.refs_0_
  43.5 0.5 collective-permute-start.5
  44.0 0.0 collective-permute-done.13.refs_3_
  44.0 0.1 collective-permute-start.1
  44.1 0.4 collective-permute-start.3
  44.5 0.7 %stage.6 = (bf16[2048,768]{1,0:T(8,128)(2,1)S(1)}, f32[8,2048]{1,0:T(8,128)S(1)}, f32[2048,128]{1,0:T(8,128)S(1)}, f32[8,1024]{1,0:T(8,128)S(1)}) custom-call(bf16[776,128]{1,0:T(8,128)(2,1)S(1)} %get-tuple-element.49.refs_0_, bf16[776,128]{1,0:T(8,128)(2,1)S(1)} %collective-permute-done.10.refs_1_, bf16[776,128]{1,0:T(8,128)(2,1)S(1)} %collective-permute-done.12.refs_2_, ...), custom_call_target="tpu_custom_call" | custom-call | tf_op jit(solution)/shard_map/stage/pallas_call | solution.py:326
  45.2 1.1 %stage.7 = (bf16[2048,768]{1,0:T(8,128)(2,1)S(1)}, f32[8,2048]{1,0:T(8,128)S(1)}, f32[2048,128]{1,0:T(8,128)S(1)}, f32[8,1024]{1,0:T(8,128)S(1)}) custom-call(bf16[776,128]{1,0:T(8,128)(2,1)S(1)} %collective-permute-done.6.refs_0_, ...), custom_call_target="tpu_custom_call", output_to_operand_aliasing={{0}: (4, {}), {1}: (5, {}), {2}: (6, {}), {3}: (7, {})} | custom-call | tf_op jit(solution)/shard_map/stage/pallas_call | solution.py:326
  46.4 1.2 %stage.8 = (bf16[2048,768]{1,0:T(8,128)(2,1)S(1)}, f32[8,2048]{1,0:T(8,128)S(1)}, f32[2048,128]{1,0:T(8,128)S(1)}, f32[8,1024]{1,0:T(8,128)S(1)}) custom-call(bf16[776,128]{1,0:T(8,128)(2,1)S(1)} %collective-permute-done.4.refs_0_, ...), custom_call_target="tpu_custom_call", output_to_operand_aliasing={{0}: (3, {}), {1}: (4, {}), {2}: (5, {}), {3}: (6, {})} | custom-call | tf_op jit(solution)/shard_map/stage/pallas_call | solution.py:326
  47.5 1.2 %stage.9 = (bf16[2048,768]{1,0:T(8,128)(2,1)S(1)}, f32[8,2048]{1,0:T(8,128)S(1)}, f32[2048,128]{1,0:T(8,128)S(1)}, f32[8,1024]{1,0:T(8,128)S(1)}) custom-call(bf16[776,128]{1,0:T(8,128)(2,1)S(1)} %collective-permute-done.refs_0_, ...), custom_call_target="tpu_custom_call", output_to_operand_aliasing={{0}: (2, {}), {1}: (3, {}), {2}: (4, {}), {3}: (5, {})} | custom-call | tf_op jit(solution)/shard_map/stage/pallas_call | solution.py:326
  48.8 1.1 %stage.10 = (bf16[2048,768]{1,0:T(8,128)(2,1)S(1)}, f32[8,2048]{1,0:T(8,128)S(1)}, f32[2048,128]{1,0:T(8,128)S(1)}, f32[8,1024]{1,0:T(8,128)S(1)}) custom-call(bf16[776,128]{1,0:T(8,128)(2,1)S(1)} %collective-permute-done.2.refs_0_, ...), custom_call_target="tpu_custom_call", output_to_operand_aliasing={{0}: (1, {}), {1}: (2, {}), {2}: (3, {}), {3}: (4, {})} | custom-call | tf_op jit(solution)/shard_map/stage/pallas_call | solution.py:326
  49.9 0.7 %stage.11 = (bf16[2048,768]{1,0:T(8,128)(2,1)S(1)}, f32[8,2048]{1,0:T(8,128)S(1)}, f32[2048,128]{1,0:T(8,128)S(1)}, f32[8,1024]{1,0:T(8,128)S(1)}, f32[16,256]{1,0:T(8,128)S(1)}) custom-call(bf16[776,128]{1,0:T(8,128)(2,1)S(1)} %collective-permute-done.1.refs_0_, ...), custom_call_target="tpu_custom_call", output_to_operand_aliasing={{0}: (2, {}), {1}: (3, {}), {2}: (4, {}), {3}: (5, {})} | custom-call | tf_op jit(solution)/shard_map/stage/pallas_call | solution.py:326
  50.7 12.3 %all_to_all.11 = f32[16,1,256]{2,1,0:T(1,128)S(1)} all-to-all(f32[16,1,256]{2,1,0:T(1,128)S(1)} %copy.25), channel_id=1, replica_groups=mesh['parts'=2,'owner'=16] {'owner'}, dimensions={0} | all-to-all | bytes 32768 | tf_op jit(solution)/shard_map/all_to_all | solution.py:442
  63.0 0.7 %finish.1 = (f32[8,128]{1,0:T(8,128)}, f32[1,64]{1,0:T(1,128)}) custom-call(f32[16,256]{1,0:T(8,128)S(1)} %bitcast.8, s32[8,128]{1,0:T(8,128)S(1)} %get-tuple-element.71.pair_ref, s32[8,128]{1,0:T(8,128)S(1)} %get-tuple-element.72.rank_ref, s32[8,128]{1,0:T(8,128)S(1)} %get-tuple-element.73.table_ref), custom_call_target="tpu_custom_call" | custom-call | tf_op jit(solution)/shard_map/finish/pallas_call | solution.py:372
  (10 shorter events, 0.0 us)
Async XLA Ops:
  4.7 8.4 %collective-permute-start.12 = (bf16[776,128]{1,0:T(8,128)(2,1)S(1)}, bf16[776,128]{1,0:T(8,128)(2,1)S(1)}, u32[]{:S(2)}, u32[]{:S(2)}) collective-permute-start(bf16[776,128]{1,0:T(8,128)(2,1)S(1)} %get-tuple-element.48), channel_id=1, source_target_pairs={{0,4},{1,5},{2,6},{3,7},{4,0},{5,1},{6,2},{7,3},{8,12},{9,13},{10,... | collective-permute-start | bytes 595976 | tf_op jit(solution)/shard_map/ppermute | solution.py:422
  7.8 11.9 %collective-permute-start.14 = (bf16[776,128]{1,0:T(8,128)(2,1)S(1)}, bf16[776,128]{1,0:T(8,128)(2,1)S(1)}, u32[]{:S(2)}, u32[]{:S(2)}) collective-permute-start(bf16[776,128]{1,0:T(8,128)(2,1)S(1)} %get-tuple-element.49.refs_0_), channel_id=1, source_target_pairs={{0,1},{1,0},{2,3},{3,2},{4,5},{5,4},{6,7},{7,6},{8,9},{9,8},{10,11... | collective-permute-start | bytes 595976 | tf_op jit(solution)/shard_map/ppermute | solution.py:425
  7.8 12.9 %collective-permute-start.10 = (bf16[776,128]{1,0:T(8,128)(2,1)S(1)}, bf16[776,128]{1,0:T(8,128)(2,1)S(1)}, u32[]{:S(2)}, u32[]{:S(2)}) collective-permute-start(bf16[776,128]{1,0:T(8,128)(2,1)S(1)} %get-tuple-element.47), channel_id=1, source_target_pairs={{0,12},{1,13},{2,14},{3,15},{4,8},{5,9},{6,10},{7,11},{8,4},{9,5},... | collective-permute-start | bytes 595976 | tf_op jit(solution)/shard_map/ppermute | solution.py:422
  10.3 15.6 %collective-permute-start.6 = (bf16[776,128]{1,0:T(8,128)(2,1)S(1)}, bf16[776,128]{1,0:T(8,128)(2,1)S(1)}, u32[]{:S(2)}, u32[]{:S(2)}) collective-permute-start(bf16[776,128]{1,0:T(8,128)(2,1)S(1)} %get-tuple-element.45), channel_id=1, source_target_pairs={{0,6},{1,7},{2,4},{3,5},{4,2},{5,3},{6,0},{7,1},{8,14},{9,15},{10,... | collective-permute-start | bytes 595976 | tf_op jit(solution)/shard_map/ppermute | solution.py:422
  11.9 13.9 %collective-permute-start.8 = (bf16[776,128]{1,0:T(8,128)(2,1)S(1)}, bf16[776,128]{1,0:T(8,128)(2,1)S(1)}, u32[]{:S(2)}, u32[]{:S(2)}) collective-permute-start(bf16[776,128]{1,0:T(8,128)(2,1)S(1)} %get-tuple-element.46), channel_id=1, source_target_pairs={{0,2},{1,3},{2,0},{3,1},{4,6},{5,7},{6,4},{7,5},{8,10},{9,11},{10,... | collective-permute-start | bytes 595976 | tf_op jit(solution)/shard_map/ppermute | solution.py:422
  13.1 25.2 %collective-permute-start.4 = (bf16[776,128]{1,0:T(8,128)(2,1)S(1)}, bf16[776,128]{1,0:T(8,128)(2,1)S(1)}, u32[]{:S(2)}, u32[]{:S(2)}) collective-permute-start(bf16[776,128]{1,0:T(8,128)(2,1)S(1)} %get-tuple-element.44), channel_id=1, source_target_pairs={{0,8},{1,9},{2,10},{3,11},{4,12},{5,13},{6,14},{7,15},{8,0},{9,1},... | collective-permute-start | bytes 595976 | tf_op jit(solution)/shard_map/ppermute | solution.py:422
  19.7 23.8 %collective-permute-start = (bf16[776,128]{1,0:T(8,128)(2,1)S(1)}, bf16[776,128]{1,0:T(8,128)(2,1)S(1)}, u32[]{:S(2)}, u32[]{:S(2)}) collective-permute-start(bf16[776,128]{1,0:T(8,128)(2,1)S(1)} %get-tuple-element.42), channel_id=1, source_target_pairs={{0,10},{1,11},{2,8},{3,9},{4,14},{5,15},{6,12},{7,13},{8,2},{9,3},... | collective-permute-start | bytes 595976 | tf_op jit(solution)/shard_map/ppermute | solution.py:422
  20.7 22.8 %collective-permute-start.2 = (bf16[776,128]{1,0:T(8,128)(2,1)S(1)}, bf16[776,128]{1,0:T(8,128)(2,1)S(1)}, u32[]{:S(2)}, u32[]{:S(2)}) collective-permute-start(bf16[776,128]{1,0:T(8,128)(2,1)S(1)} %get-tuple-element.43), channel_id=1, source_target_pairs={{0,14},{1,15},{2,12},{3,13},{4,10},{5,11},{6,8},{7,9},{8,6},{9,7},... | collective-permute-start | bytes 595976 | tf_op jit(solution)/shard_map/ppermute | solution.py:422
  25.8 18.1 %collective-permute-start.13 = (bf16[776,128]{1,0:T(8,128)(2,1)S(1)}, bf16[776,128]{1,0:T(8,128)(2,1)S(1)}, u32[]{:S(2)}, u32[]{:S(2)}) collective-permute-start(bf16[776,128]{1,0:T(8,128)(2,1)S(1)} %collective-permute-done.12.refs_2_), channel_id=1, source_target_pairs={{0,1},{1,0},{2,3},{3,2},{4,5},{5,4},{6,7},{7,6},{8,9},{9,8},{10,11... | collective-permute-start | bytes 595976 | tf_op jit(solution)/shard_map/ppermute | solution.py:425
  25.9 18.2 %collective-permute-start.11 = (bf16[776,128]{1,0:T(8,128)(2,1)S(1)}, bf16[776,128]{1,0:T(8,128)(2,1)S(1)}, u32[]{:S(2)}, u32[]{:S(2)}) collective-permute-start(bf16[776,128]{1,0:T(8,128)(2,1)S(1)} %collective-permute-done.10.refs_1_), channel_id=1, source_target_pairs={{0,1},{1,0},{2,3},{3,2},{4,5},{5,4},{6,7},{7,6},{8,9},{9,8},{10,11... | collective-permute-start | bytes 595976 | tf_op jit(solution)/shard_map/ppermute | solution.py:425
  38.3 8.1 %collective-permute-start.7 = (bf16[776,128]{1,0:T(8,128)(2,1)S(1)}, bf16[776,128]{1,0:T(8,128)(2,1)S(1)}, u32[]{:S(2)}, u32[]{:S(2)}) collective-permute-start(bf16[776,128]{1,0:T(8,128)(2,1)S(1)} %collective-permute-done.6.refs_0_), channel_id=1, source_target_pairs={{0,1},{1,0},{2,3},{3,2},{4,5},{5,4},{6,7},{7,6},{8,9},{9,8},{10,11... | collective-permute-start | bytes 595976 | tf_op jit(solution)/shard_map/ppermute | solution.py:425
  43.5 2.9 %collective-permute-start.9 = (bf16[776,128]{1,0:T(8,128)(2,1)S(1)}, bf16[776,128]{1,0:T(8,128)(2,1)S(1)}, u32[]{:S(2)}, u32[]{:S(2)}) collective-permute-start(bf16[776,128]{1,0:T(8,128)(2,1)S(1)} %collective-permute-done.8.refs_1_), channel_id=1, source_target_pairs={{0,1},{1,0},{2,3},{3,2},{4,5},{5,4},{6,7},{7,6},{8,9},{9,8},{10,11... | collective-permute-start | bytes 595976 | tf_op jit(solution)/shard_map/ppermute | solution.py:425
  43.5 4.1 %collective-permute-start.5 = (bf16[776,128]{1,0:T(8,128)(2,1)S(1)}, bf16[776,128]{1,0:T(8,128)(2,1)S(1)}, u32[]{:S(2)}, u32[]{:S(2)}) collective-permute-start(bf16[776,128]{1,0:T(8,128)(2,1)S(1)} %collective-permute-done.4.refs_0_), channel_id=1, source_target_pairs={{0,1},{1,0},{2,3},{3,2},{4,5},{5,4},{6,7},{7,6},{8,9},{9,8},{10,11... | collective-permute-start | bytes 595976 | tf_op jit(solution)/shard_map/ppermute | solution.py:425
  44.0 5.9 %collective-permute-start.1 = (bf16[776,128]{1,0:T(8,128)(2,1)S(1)}, bf16[776,128]{1,0:T(8,128)(2,1)S(1)}, u32[]{:S(2)}, u32[]{:S(2)}) collective-permute-start(bf16[776,128]{1,0:T(8,128)(2,1)S(1)} %collective-permute-done.refs_0_), channel_id=1, source_target_pairs={{0,1},{1,0},{2,3},{3,2},{4,5},{5,4},{6,7},{7,6},{8,9},{9,8},{10,11... | collective-permute-start | bytes 595976 | tf_op jit(solution)/shard_map/ppermute | solution.py:425
  44.1 5.9 %collective-permute-start.3 = (bf16[776,128]{1,0:T(8,128)(2,1)S(1)}, bf16[776,128]{1,0:T(8,128)(2,1)S(1)}, u32[]{:S(2)}, u32[]{:S(2)}) collective-permute-start(bf16[776,128]{1,0:T(8,128)(2,1)S(1)} %collective-permute-done.2.refs_0_), channel_id=1, source_target_pairs={{0,1},{1,0},{2,3},{3,2},{4,5},{5,4},{6,7},{7,6},{8,9},{9,8},{10,11... | collective-permute-start | bytes 595976 | tf_op jit(solution)/shard_map/ppermute | solution.py:425
